TPU v7x, 512 devices: a whole 4x8x8 slice. The times are simulated.
512 devices in a mesh: flow: 8 (over y), cross: 64 (over x, z, core).
Axes of the slice: x: 4, y: 8, z: 8, core: 2. Of those that a mesh axis runs over, the one named last changes fastest.
Arguments:
- conc_old: float32 [8, 64, 64, 8, 128], P('flow', 'cross'), may hold values from 0.05 to 2
- face_flux: float32 [8, 64, 8, 128, 128], P('flow', 'cross'), may hold values from 0 to 0.01484375
- block_inverse: float32 [8, 64, 8, 128, 128], P('flow', 'cross'), may hold values from 0 to 1
- upstream_block: int32 [8, 64, 8], P('flow', 'cross'), may hold values from 0 to 6, as said below
- send_cells: int32 [8, 64, 64, 128], P('flow', 'cross'), may hold values from 0 to 1023
- send_count: int32 [8, 64, 64], P('flow', 'cross'), may hold values from 0 to 128, as said below
- recv_cells: int32 [8, 64, 64, 128], P('flow', 'cross'), may hold values from 0 to 1023
- recv_coef: float32 [8, 64, 64, 128], P('flow', 'cross'), may hold values from 0.1 to 1
Outputs:
- conc_new: float32 [8, 64, 64, 8, 128], P('flow', 'cross')
Inputs may be any that keep to these rules, and one draw needn't show every extreme that they name: For j >= 1, upstream_block[f, q, j] < j; entry 0 is unused and is 0; block 7 is fed by block 6. `send_count`: entry [f, s, d] counts the live slots from device s to device d of the cross axis; a device sends nothing to itself; every device sends a full 128 to at least one other device and receives a full 128 from at least one.
All inputs are finite; a program needn't handle non-finite values.
Results may differ from a plain program's by a relative error of at most 0.0003.
Values sent between devices are 32-bit elements; how exact they have to be, the bound alone decides.
A program may use at most 64 MiB of HBM per device.

v0:
```python
import jax
import jax.numpy as jnp
from jax import lax
from jax.sharding import PartitionSpec as P


def from_behind(shard, axis, by):
    count = lax.axis_size(axis)
    pairs = [(i, i + by) for i in range(count) if 0 <= i + by < count]
    return lax.ppermute(shard, axis, pairs)


def matmul(left, right):
    return jnp.dot(left, right, precision=lax.Precision.HIGHEST, preferred_element_type=jnp.float32)


def upwind_sweep(incoming, source, couplings, inverses, feeders):
    blocks = source.shape[1]
    head_block = matmul(source[:, 0] + matmul(incoming, couplings[0]), inverses[0])
    solved_all = jnp.zeros_like(source).at[:, 0].set(head_block)

    def advance(block_id, solved_all):
        block_id = block_id.astype(jnp.int32)
        feeder = lax.dynamic_index_in_dim(solved_all, feeders[block_id], 1, keepdims=False)
        block_source = lax.dynamic_index_in_dim(source, block_id, 1, keepdims=False)
        coupling = lax.dynamic_index_in_dim(couplings, block_id, 0, keepdims=False)
        inverse = lax.dynamic_index_in_dim(inverses, block_id, 0, keepdims=False)
        solved = matmul(block_source + matmul(feeder, coupling), inverse)
        return lax.dynamic_update_index_in_dim(solved_all, solved, block_id, 1)

    return lax.fori_loop(1, blocks, advance, solved_all)


def on_device(
    conc_old,
    face_flux,
    block_inverse,
    upstream_block,
    send_cells,
    send_count,
    recv_cells,
    recv_coef,
):
    current = conc_old[0, 0]
    members, blocks, cells = current.shape
    couplings = face_flux[0, 0]
    inverses = block_inverse[0, 0]
    feeders = upstream_block[0, 0]
    flat_conc = current.reshape(members, -1)
    n_cross, slot_count = (send_cells.shape[2], send_cells.shape[3])
    send_index = send_cells[0, 0].reshape(-1)
    picked = flat_conc[:, send_index].reshape(members, n_cross, slot_count)
    live_slot = (
        lax.broadcasted_iota(jnp.int32, (n_cross, slot_count), 1) < send_count[0, 0][:, None]
    )
    outgoing = jnp.where(live_slot[None], picked, 0.0)
    targets = recv_cells[0, 0].reshape(-1)
    weights = recv_coef[0, 0]
    arrived = lax.all_to_all(outgoing, "cross", split_axis=1, concat_axis=1, tiled=True)
    weighted = arrived * weights[None]
    empty = jnp.zeros((arrived.shape[0], flat_conc.shape[1]), jnp.float32)
    lateral = empty.at[:, targets].add(weighted.reshape(arrived.shape[0], -1))
    source = current + lateral.reshape(current.shape)
    zero_in = jnp.zeros((members, cells), jnp.float32)
    incoming = zero_in
    for round_id in range(lax.axis_size("flow") - 1):
        solved = upwind_sweep(incoming, source, couplings, inverses, feeders)
        incoming = from_behind(solved[:, -1], "flow", 1)
    solved = upwind_sweep(incoming, source, couplings, inverses, feeders)
    return solved[None, None]


def solution(mesh):
    placed = (
        P("flow", "cross", None, None, None),
        P("flow", "cross", None, None, None),
        P("flow", "cross", None, None, None),
        P("flow", "cross", None),
        P("flow", "cross", None, None),
        P("flow", "cross", None),
        P("flow", "cross", None, None),
        P("flow", "cross", None, None),
    )
    return jax.shard_map(
        on_device,
        mesh=mesh,
        in_specs=placed,
        out_specs=P("flow", "cross", None, None, None),
        check_vma=False,
    )
```

profile of v0, /device:TPU:32, one launch (start us, length us, event | category | flops | bytes accessed | tf_op | source)
XLA Modules:
  0.0 369.6 jit_solution(9489297861093187056)
XLA Ops:
  0.0 1.1 copy.23
  1.2 0.8 compare_select_fusion
  2.0 27.8 %gather_fusion = f32[8192,64]{1,0:T(8,128)} fusion(f32[64,1024]{0,1:T(8,128)S(1)} %bitcast.371, s32[8192]{0:T(1024)S(1)} %broadcast_clamp_fusion), kind=kCustom, calls=%fused_computation | custom fusion | bytes 4227072 | tf_op jit(solution)/shard_map/gather | solution.py:52
  29.7 2.8 copy.24
  32.7 1.6 broadcast_select_fusion
  34.3 13.9 %all-to-all-start = ((f32[64,64,128]{2,0,1:T(8,128)}), f32[64,64,128]{2,0,1:T(8,128)S(1)}, u32[]{:S(2)}, u32[]{:S(2)}) async-start(f32[64,64,128]{2,0,1:T(8,128)} %broadcast_select_fusion), calls=%async_computation | async-start | bytes 4194304 | tf_op jit(solution)/shard_map/all_to_all | solution.py:59
  48.3 51.1 %all-to-all-done = f32[64,64,128]{2,0,1:T(8,128)S(1)} async-done(((f32[64,64,128]{2,0,1:T(8,128)}), f32[64,64,128]{2,0,1:T(8,128)S(1)}, u32[]{:S(2)}, u32[]{:S(2)}) %all-to-all-start) | async-done | bytes 2097184 | tf_op jit(solution)/shard_map/all_to_all | solution.py:59
  99.4 1.3 copy-done.2
  100.7 1.8 bitcast_bitcast_fusion
  102.5 2.7 copy.26
  105.2 44.5 %scatter_custom_fusion = f32[64,1024]{0,1:T(8,128)S(1)} fusion(s32[8192]{0:T(1024)S(1)} %bitcast.394, f32[8192,64]{1,0:T(8,128)} %copy.26, f32[]{:T(128)} %constant.557.clone.1), kind=kCustom, calls=%fused_computation.111 | custom fusion | flops 524288 | bytes 262656 | tf_op jit(solution)/shard_map/scatter-add | solution.py:62
  149.9 1.0 bitcast_add_fusion
  151.4 20.6 %while.128 = (s32[]{:T(128)}, f32[64,8,128]{2,0,1:T(8,128)S(1)}, f32[64,8,128]{2,0,1:T(8,128)S(1)}, s32[8]{0:T(128)S(1)}, f32[8,128,128]{2,1,0:T(8,128)S(1)}, /*...) while((s32[]{:T(128)}, f32[64,8,128]{2,0,1:T(8,128)S(1)}, ...), condition=%wide.region_2.3_spmd, body=%wide.region_1.2_spmd.sunk | while | flops 25174024 | bytes 297661 | solution.py:31
  151.4 0.6 dynamic_slice.550
  154.3 0.6 dynamic_slice.550
  172.0 2.6 collective-permute-start
  174.6 4.4 %collective-permute-done = f32[64,128]{1,0:T(8,128)S(1)} collective-permute-done((f32[64,128]{1,0:T(8,128)S(1)}, f32[64,128]{1,0:T(8,128)S(1)}, u32[]{:S(2)}, u32[]{:S(2)}) %collective-permute-start) | collective-permute-done | bytes 32800 | tf_op jit(solution)/shard_map/ppermute | solution.py:10
  179.5 20.6 %while.129 = (s32[]{:T(128)}, f32[64,8,128]{2,0,1:T(8,128)S(1)}, f32[64,8,128]{2,0,1:T(8,128)S(1)}, s32[8]{0:T(128)S(1)}, f32[8,128,128]{2,1,0:T(8,128)S(1)}, /*...) while((s32[]{:T(128)}, f32[64,8,128]{2,0,1:T(8,128)S(1)}, ...), condition=%wide.region_4.5_spmd, body=%wide.region_3.4_spmd.sunk | while | flops 25174024 | bytes 297661 | solution.py:31
  200.1 1.9 collective-permute-start.1
  202.0 5.1 %collective-permute-done.1 = f32[64,128]{1,0:T(8,128)S(1)} collective-permute-done((f32[64,128]{1,0:T(8,128)S(1)}, f32[64,128]{1,0:T(8,128)S(1)}, u32[]{:S(2)}, u32[]{:S(2)}) %collective-permute-start.1) | collective-permute-done | bytes 32800 | tf_op jit(solution)/shard_map/ppermute | solution.py:10
  207.5 20.6 %while.130 = (s32[]{:T(128)}, f32[64,8,128]{2,0,1:T(8,128)S(1)}, f32[64,8,128]{2,0,1:T(8,128)S(1)}, s32[8]{0:T(128)S(1)}, f32[8,128,128]{2,1,0:T(8,128)S(1)}, /*...) while((s32[]{:T(128)}, f32[64,8,128]{2,0,1:T(8,128)S(1)}, ...), condition=%wide.region_6.7_spmd, body=%wide.region_5.6_spmd.sunk | while | flops 25174024 | bytes 297661 | solution.py:31
  228.2 1.9 collective-permute-start.2
  230.1 5.1 %collective-permute-done.2 = f32[64,128]{1,0:T(8,128)S(1)} collective-permute-done((f32[64,128]{1,0:T(8,128)S(1)}, f32[64,128]{1,0:T(8,128)S(1)}, u32[]{:S(2)}, u32[]{:S(2)}) %collective-permute-start.2) | collective-permute-done | bytes 32800 | tf_op jit(solution)/shard_map/ppermute | solution.py:10
  235.6 20.7 %while.131 = (s32[]{:T(128)}, f32[64,8,128]{2,0,1:T(8,128)S(1)}, f32[64,8,128]{2,0,1:T(8,128)S(1)}, s32[8]{0:T(128)S(1)}, f32[8,128,128]{2,1,0:T(8,128)S(1)}, /*...) while((s32[]{:T(128)}, f32[64,8,128]{2,0,1:T(8,128)S(1)}, ...), condition=%wide.region_8.9_spmd, body=%wide.region_7.8_spmd.sunk | while | flops 25174024 | bytes 297661 | solution.py:31
  235.7 0.6 dynamic_slice.565
  238.6 0.6 dynamic_slice.565
  256.3 1.9 collective-permute-start.3
  258.2 5.1 %collective-permute-done.3 = f32[64,128]{1,0:T(8,128)S(1)} collective-permute-done((f32[64,128]{1,0:T(8,128)S(1)}, f32[64,128]{1,0:T(8,128)S(1)}, u32[]{:S(2)}, u32[]{:S(2)}) %collective-permute-start.3) | collective-permute-done | bytes 32800 | tf_op jit(solution)/shard_map/ppermute | solution.py:10
  263.7 20.6 %while.132 = (s32[]{:T(128)}, f32[64,8,128]{2,0,1:T(8,128)S(1)}, f32[64,8,128]{2,0,1:T(8,128)S(1)}, s32[8]{0:T(128)S(1)}, f32[8,128,128]{2,1,0:T(8,128)S(1)}, /*...) while((s32[]{:T(128)}, f32[64,8,128]{2,0,1:T(8,128)S(1)}, ...), condition=%wide.region_10.11_spmd, body=%wide.region_9.10_spmd.sunk | while | flops 25174024 | bytes 297661 | solution.py:31
  284.4 1.9 collective-permute-start.4
  286.3 5.1 %collective-permute-done.4 = f32[64,128]{1,0:T(8,128)S(1)} collective-permute-done((f32[64,128]{1,0:T(8,128)S(1)}, f32[64,128]{1,0:T(8,128)S(1)}, u32[]{:S(2)}, u32[]{:S(2)}) %collective-permute-start.4) | collective-permute-done | bytes 32800 | tf_op jit(solution)/shard_map/ppermute | solution.py:10
  291.8 20.6 %while.133 = (s32[]{:T(128)}, f32[64,8,128]{2,0,1:T(8,128)S(1)}, f32[64,8,128]{2,0,1:T(8,128)S(1)}, s32[8]{0:T(128)S(1)}, f32[8,128,128]{2,1,0:T(8,128)S(1)}, /*...) while((s32[]{:T(128)}, f32[64,8,128]{2,0,1:T(8,128)S(1)}, ...), condition=%wide.region_12.13_spmd, body=%wide.region_11.12_spmd.sunk | while | flops 25174024 | bytes 297661 | solution.py:31
  297.8 0.6 dynamic_slice.575
  300.7 0.6 dynamic_slice.575
  303.7 0.6 dynamic_slice.575
  306.6 0.6 dynamic_slice.575
  309.6 0.6 dynamic_slice.575
  312.5 1.9 collective-permute-start.5
  314.4 5.1 %collective-permute-done.5 = f32[64,128]{1,0:T(8,128)S(1)} collective-permute-done((f32[64,128]{1,0:T(8,128)S(1)}, f32[64,128]{1,0:T(8,128)S(1)}, u32[]{:S(2)}, u32[]{:S(2)}) %collective-permute-start.5) | collective-permute-done | bytes 32800 | tf_op jit(solution)/shard_map/ppermute | solution.py:10
  319.9 20.6 %while.134 = (s32[]{:T(128)}, f32[64,8,128]{2,0,1:T(8,128)S(1)}, f32[64,8,128]{2,0,1:T(8,128)S(1)}, s32[8]{0:T(128)S(1)}, f32[8,128,128]{2,1,0:T(8,128)S(1)}, /*...) while((s32[]{:T(128)}, f32[64,8,128]{2,0,1:T(8,128)S(1)}, ...), condition=%wide.region_14.15_spmd, body=%wide.region_13.14_spmd.sunk | while | flops 25174024 | bytes 297661 | solution.py:31
  328.8 0.6 dynamic_slice.580
  331.8 0.6 dynamic_slice.580
  334.7 0.6 dynamic_slice.580
  337.7 0.6 dynamic_slice.580
  340.6 1.9 collective-permute-start.6
  342.5 5.1 %collective-permute-done.6 = f32[64,128]{1,0:T(8,128)S(1)} collective-permute-done((f32[64,128]{1,0:T(8,128)S(1)}, f32[64,128]{1,0:T(8,128)S(1)}, u32[]{:S(2)}, u32[]{:S(2)}) %collective-permute-start.6) | collective-permute-done | bytes 32800 | tf_op jit(solution)/shard_map/ppermute | solution.py:10
  348.0 20.6 %while.135 = (s32[]{:T(128)}, f32[64,8,128]{2,0,1:T(8,128)S(1)}, f32[64,8,128]{2,0,1:T(8,128)S(1)}, s32[8]{0:T(128)S(1)}, f32[8,128,128]{2,1,0:T(8,128)S(1)}, /*...) while((s32[]{:T(128)}, f32[64,8,128]{2,0,1:T(8,128)S(1)}, ...), condition=%wide.region_16.17_spmd, body=%wide.region_15.16_spmd.sunk | while | flops 25174024 | bytes 297661 | solution.py:31
  368.7 0.9 copy.36
  (203 shorter events, 50.2 us)
Async XLA Ops:
  29.7 2.8 copy-start.5
  34.3 13.9 %copy-start.4 = (s32[1,1,64,128]{3,2,1,0:T(8,128)S(1)}, s32[1,1,64,128]{3,2,1,0:T(8,128)}, u32[]{:S(2)}) copy-start(s32[1,1,64,128]{3,2,1,0:T(8,128)} %param.46) | copy-start | bytes 98308
  34.3 66.4 %copy-start.3 = (f32[1,1,64,128]{3,2,1,0:T(8,128)S(1)}, f32[1,1,64,128]{3,2,1,0:T(8,128)}, u32[]{:S(2)}) copy-start(f32[1,1,64,128]{3,2,1,0:T(8,128)} %param.47) | copy-start | bytes 98308
  34.3 65.1 %all-to-all-start = ((f32[64,64,128]{2,0,1:T(8,128)}), f32[64,64,128]{2,0,1:T(8,128)S(1)}, u32[]{:S(2)}, u32[]{:S(2)}) async-start(f32[64,64,128]{2,0,1:T(8,128)} %broadcast_select_fusion), calls=%async_computation | async-start | bytes 4194304 | tf_op jit(solution)/shard_map/all_to_all | solution.py:59
  99.4 1.3 copy-start.2
  105.2 45.7 %copy-start = (f32[1,1,8,128,128]{4,3,2,1,0:T(8,128)S(1)}, f32[1,1,8,128,128]{4,3,2,1,0:T(8,128)}, u32[]{:S(2)}) copy-start(f32[1,1,8,128,128]{4,3,2,1,0:T(8,128)} %param.41) | copy-start | bytes 1572868
  105.2 45.9 %copy-start.1 = (f32[1,1,8,128,128]{4,3,2,1,0:T(8,128)S(1)}, f32[1,1,8,128,128]{4,3,2,1,0:T(8,128)}, u32[]{:S(2)}) copy-start(f32[1,1,8,128,128]{4,3,2,1,0:T(8,128)} %param.42) | copy-start | bytes 1572868
  105.2 46.2 %copy-start.6 = (s32[1,1,8]{2,1,0:T(1,128)S(1)}, s32[1,1,8]{2,1,0:T(1,128)}, u32[]{:S(2)}) copy-start(s32[1,1,8]{2,1,0:T(1,128)} %param.43) | copy-start | bytes 100
  172.0 7.0 %collective-permute-start = (f32[64,128]{1,0:T(8,128)S(1)}, f32[64,128]{1,0:T(8,128)S(1)}, u32[]{:S(2)}, u32[]{:S(2)}) collective-permute-start(f32[64,128]{1,0:T(8,128)S(1)} %slice_bitcast_fusion.7), channel_id=1, source_target_pairs={{0,64},{64,128},{128,192},{192,256},{256,320},{320,384},{384,448},... | collective-permute-start | bytes 98312 | tf_op jit(solution)/shard_map/ppermute | solution.py:10
  200.1 7.0 %collective-permute-start.1 = (f32[64,128]{1,0:T(8,128)S(1)}, f32[64,128]{1,0:T(8,128)S(1)}, u32[]{:S(2)}, u32[]{:S(2)}) collective-permute-start(f32[64,128]{1,0:T(8,128)S(1)} %slice_bitcast_fusion.6), channel_id=1, source_target_pairs={{0,64},{64,128},{128,192},{192,256},{256,320},{320,384},{384,448},... | collective-permute-start | bytes 98312 | tf_op jit(solution)/shard_map/ppermute | solution.py:10
  228.2 7.0 %collective-permute-start.2 = (f32[64,128]{1,0:T(8,128)S(1)}, f32[64,128]{1,0:T(8,128)S(1)}, u32[]{:S(2)}, u32[]{:S(2)}) collective-permute-start(f32[64,128]{1,0:T(8,128)S(1)} %slice_bitcast_fusion.5), channel_id=1, source_target_pairs={{0,64},{64,128},{128,192},{192,256},{256,320},{320,384},{384,448},... | collective-permute-start | bytes 98312 | tf_op jit(solution)/shard_map/ppermute | solution.py:10
  256.3 7.0 %collective-permute-start.3 = (f32[64,128]{1,0:T(8,128)S(1)}, f32[64,128]{1,0:T(8,128)S(1)}, u32[]{:S(2)}, u32[]{:S(2)}) collective-permute-start(f32[64,128]{1,0:T(8,128)S(1)} %slice_bitcast_fusion.4), channel_id=1, source_target_pairs={{0,64},{64,128},{128,192},{192,256},{256,320},{320,384},{384,448},... | collective-permute-start | bytes 98312 | tf_op jit(solution)/shard_map/ppermute | solution.py:10
  284.4 7.0 %collective-permute-start.4 = (f32[64,128]{1,0:T(8,128)S(1)}, f32[64,128]{1,0:T(8,128)S(1)}, u32[]{:S(2)}, u32[]{:S(2)}) collective-permute-start(f32[64,128]{1,0:T(8,128)S(1)} %slice_bitcast_fusion.3), channel_id=1, source_target_pairs={{0,64},{64,128},{128,192},{192,256},{256,320},{320,384},{384,448},... | collective-permute-start | bytes 98312 | tf_op jit(solution)/shard_map/ppermute | solution.py:10
  312.5 7.0 %collective-permute-start.5 = (f32[64,128]{1,0:T(8,128)S(1)}, f32[64,128]{1,0:T(8,128)S(1)}, u32[]{:S(2)}, u32[]{:S(2)}) collective-permute-start(f32[64,128]{1,0:T(8,128)S(1)} %slice_bitcast_fusion.2), channel_id=1, source_target_pairs={{0,64},{64,128},{128,192},{192,256},{256,320},{320,384},{384,448},... | collective-permute-start | bytes 98312 | tf_op jit(solution)/shard_map/ppermute | solution.py:10
  340.6 7.0 %collective-permute-start.6 = (f32[64,128]{1,0:T(8,128)S(1)}, f32[64,128]{1,0:T(8,128)S(1)}, u32[]{:S(2)}, u32[]{:S(2)}) collective-permute-start(f32[64,128]{1,0:T(8,128)S(1)} %slice_bitcast_fusion.1), channel_id=1, source_target_pairs={{0,64},{64,128},{128,192},{192,256},{256,320},{320,384},{384,448},... | collective-permute-start | bytes 98312 | tf_op jit(solution)/shard_map/ppermute | solution.py:10
where the time goes:
time: 372 us; the launch traced here: 370 us
  loops' own time  111 us (30%)
  waiting for transfers between devices  86.1 us (23%)
  local copies, waits for them, and re-layouts  69.9 us (19%)
  other arithmetic  49.8 us (13%)
  starting transfers between devices  28 us (8%)
  matrix products  24.4 us (7%)
    another operation x8, loops' own time, upwind_sweep(): return lax.fori_loop(1, blocks, advance, solved_all)  111 us
    all_to_all x1, waiting for transfers between devices, on_device(): lax.all_to_all(outgoing, 'cross', split_axis=1, concat_axis=1, tiled=True)  51.1 us
    scatter-add x1, other arithmetic, on_device(): lateral = empty.at[:, targets].add(weighted.reshape(arrived.shape[0], -1))  44.5 us
    ppermute x7, waiting for transfers between devices, from_behind(): return lax.ppermute(shard, axis, pairs)  35 us
    dynamic_slice x56, local copies, waits for them, and re-layouts, advance(): feeders[block_id]  32.9 us
    gather x1, local copies, waits for them, and re-layouts, on_device(): picked = flat_conc[:, send_index].reshape(members, n_cross, slot_count)  27.8 us
    dot_general x128, matrix products, matmul(): jnp.dot(left, right, precision=lax.Precision.HIGHEST, preferred_element_t...  24.4 us
    ppermute x7, starting transfers between devices, from_behind(): return lax.ppermute(shard, axis, pairs)  14.1 us
  transfers between devices with their start and end apart: 8, of which 8 were waited for; matrix products, arithmetic and copies ran while one was open for 0% of the time, Pallas kernels for 0%

commit v1 on v0

v1 whole, which is shorter than its diff:
```python
import jax
import jax.numpy as jnp
from jax import lax
from jax.experimental import pallas as pl
from jax.experimental.pallas import tpu as pltpu
from jax.sharding import PartitionSpec as P

MESH = pl.DeviceIdType.MESH
E, NB, B = 64, 8, 128
CELLS = NB * B
N_FLOW = 8


def split(value):
    high = value.astype(jnp.bfloat16)
    low = (value - high.astype(jnp.float32)).astype(jnp.bfloat16)
    return high, low


def dot(left, right):
    return jnp.dot(left, right, preferred_element_type=jnp.float32)


def dot3(left, right):
    left_high, left_low = left
    right_high, right_low = right
    return dot(left_high, right_high) + dot(left_low, right_high) + dot(left_high, right_low)


def build_response(feeders, flux_ref, inverse_ref, resp_high, resp_low):
    resp_high[0] = jnp.zeros((CELLS + B, B), jnp.bfloat16)
    resp_low[0] = jnp.zeros((CELLS + B, B), jnp.bfloat16)
    first = split(dot3(split(flux_ref[0]), split(inverse_ref[0])))
    resp_high[0, pl.ds(CELLS, B), :] = first[0]
    resp_low[0, pl.ds(CELLS, B), :] = first[1]
    own = split(inverse_ref[0])
    resp_high[0, pl.ds(0, B), :] = own[0]
    resp_low[0, pl.ds(0, B), :] = own[1]

    def advance(j, carry):
        feeder = feeders[j]
        own = split(inverse_ref[j])
        step = split(dot3(split(flux_ref[j]), own))
        rows = split(dot3((resp_high[feeder], resp_low[feeder]), step))
        resp_high[j] = rows[0]
        resp_low[j] = rows[1]
        spot = pl.ds(pl.multiple_of(j * B, B), B)
        resp_high[j, spot, :] = own[0]
        resp_low[j, spot, :] = own[1]
        return carry

    lax.fori_loop(1, NB, advance, 0)


def sweep_kernel(feeders, source_ref, flux_ref, inverse_ref, out_ref,
                 resp_high, resp_low, src, local, incoming, outlet, send_sem, recv_sem):
    me = lax.axis_index("flow")
    right, left = lax.rem(me + 1, N_FLOW), lax.rem(me + N_FLOW - 1, N_FLOW)
    barrier = pltpu.get_barrier_semaphore()
    for neighbour in (left, right):
        pl.semaphore_signal(barrier, inc=1, device_id={"flow": neighbour}, device_id_type=MESH)
    build_response(feeders, flux_ref, inverse_ref, resp_high, resp_low)
    for b in range(NB):
        high, low = split(source_ref[:, b, :])
        src[pl.ds(0, E), pl.ds(b * B, B)] = high
        src[pl.ds(E, E), pl.ds(b * B, B)] = low

    def solve(j):
        both = dot(src[...], resp_high[j, pl.ds(0, CELLS), :])
        return both[:E] + both[E:] + dot(src[pl.ds(0, E), :], resp_low[j, pl.ds(0, CELLS), :])

    def entering(j, parts):
        return dot3(parts, (resp_high[j, pl.ds(CELLS, B), :], resp_low[j, pl.ds(CELLS, B), :]))

    pl.semaphore_wait(barrier, 2)
    copy = pltpu.make_async_remote_copy(
        src_ref=outlet, dst_ref=incoming, send_sem=send_sem, recv_sem=recv_sem,
        device_id={"flow": right}, device_id_type=MESH)
    last = solve(NB - 1)

    @pl.when(me == 0)
    def _():
        outlet[...] = last
        copy.start()
        incoming[...] = jnp.zeros_like(incoming)

    for j in range(NB - 1):
        local[j] = solve(j)

    @pl.when(me > 0)
    def _():
        copy.wait_recv()
        outlet[...] = last + entering(NB - 1, split(incoming[...]))

        @pl.when(me < N_FLOW - 1)
        def _():
            copy.start()

    out_ref[:, NB - 1, :] = outlet[...]
    parts = split(incoming[...])
    for j in range(NB - 1):
        out_ref[:, j, :] = local[j] + entering(j, parts)

    @pl.when(me < N_FLOW - 1)
    def _():
        copy.wait_send()


def sweep(source, couplings, inverses, feeders):
    vmem = pl.BlockSpec(memory_space=pltpu.VMEM)
    return pl.pallas_call(
        sweep_kernel,
        out_shape=jax.ShapeDtypeStruct((E, NB, B), jnp.float32),
        in_specs=[pl.BlockSpec(memory_space=pltpu.SMEM), vmem, vmem, vmem],
        out_specs=vmem,
        scratch_shapes=[
            pltpu.VMEM((NB, CELLS + B, B), jnp.bfloat16),
            pltpu.VMEM((NB, CELLS + B, B), jnp.bfloat16),
            pltpu.VMEM((2 * E, CELLS), jnp.bfloat16),
            pltpu.VMEM((NB, E, B), jnp.float32),
            pltpu.VMEM((E, B), jnp.float32),
            pltpu.VMEM((E, B), jnp.float32),
            pltpu.SemaphoreType.DMA,
            pltpu.SemaphoreType.DMA,
        ],
        compiler_params=pltpu.CompilerParams(collective_id=0, has_side_effects=True),
        name="sweep",
    )(feeders, source, couplings, inverses)


def on_device(conc_old, face_flux, block_inverse, upstream_block, send_cells, send_count, recv_cells, recv_coef):
    current = conc_old[0, 0]
    members = current.shape[0]
    flat_conc = current.reshape(members, -1)
    n_cross, slot_count = (send_cells.shape[2], send_cells.shape[3])
    send_index = send_cells[0, 0].reshape(-1)
    picked = flat_conc[:, send_index].reshape(members, n_cross, slot_count)
    live_slot = (
        lax.broadcasted_iota(jnp.int32, (n_cross, slot_count), 1) < send_count[0, 0][:, None]
    )
    outgoing = jnp.where(live_slot[None], picked, 0.0)
    targets = recv_cells[0, 0].reshape(-1)
    weights = recv_coef[0, 0]
    arrived = lax.all_to_all(outgoing, "cross", split_axis=1, concat_axis=1, tiled=True)
    weighted = arrived * weights[None]
    empty = jnp.zeros((arrived.shape[0], flat_conc.shape[1]), jnp.float32)
    lateral = empty.at[:, targets].add(weighted.reshape(arrived.shape[0], -1))
    source = current + lateral.reshape(current.shape)
    return sweep(source, face_flux[0, 0], block_inverse[0, 0], upstream_block[0, 0])[None, None]


def solution(mesh):
    placed = (
        P("flow", "cross", None, None, None),
        P("flow", "cross", None, None, None),
        P("flow", "cross", None, None, None),
        P("flow", "cross", None),
        P("flow", "cross", None, None),
        P("flow", "cross", None),
        P("flow", "cross", None, None),
        P("flow", "cross", None, None),
    )
    return jax.shard_map(
        on_device,
        mesh=mesh,
        in_specs=placed,
        out_specs=P("flow", "cross", None, None, None),
        check_vma=False,
    )
```

time: 372 us -> 181 us (0.49)
  the two profiles are of different devices: /device:TPU:32 before, /device:TPU:56 now
where the time goes in v1:
time: 181 us
  waiting for transfers between devices  51.1 us (28%)
  other arithmetic  49.5 us (27%)
  local copies, waits for them, and re-layouts  37.8 us (21%)
  Pallas kernels  28.4 us (16%)
  starting transfers between devices  13.9 us (8%)
    all_to_all x1, waiting for transfers between devices, on_device(): lax.all_to_all(outgoing, 'cross', split_axis=1, concat_axis=1, tiled=True)  51.1 us
    scatter-add x1, other arithmetic, on_device(): lateral = empty.at[:, targets].add(weighted.reshape(arrived.shape[0], -1))  44.4 us
    pallas_call x1, Pallas kernels, sweep(): pl.pallas_call(sweep_kernel, out_shape=jax.ShapeDtypeStruct((E, NB, B), j...  28.4 us
    gather x1, local copies, waits for them, and re-layouts, on_device(): picked = flat_conc[:, send_index].reshape(members, n_cross, slot_count)  27.8 us
    all_to_all x1, starting transfers between devices, on_device(): lax.all_to_all(outgoing, 'cross', split_axis=1, concat_axis=1, tiled=True)  13.9 us
    unnamed x12, local copies, waits for them, and re-layouts  4.16 us
  transfers between devices with their start and end apart: 1, of which 1 were waited for; matrix products, arithmetic and copies ran while one was open for 0% of the time, Pallas kernels for 0%

profile of v1, /device:TPU:56, one launch (start us, length us, event | category | flops | bytes accessed | tf_op | source)
XLA Modules:
  0.0 180.7 jit_solution(12804665462729657811)
XLA Ops:
  0.0 1.1 copy.14
  1.2 0.8 compare_select_fusion
  2.0 27.8 %gather_fusion = f32[8192,64]{1,0:T(8,128)} fusion(f32[64,1024]{0,1:T(8,128)S(1)} %bitcast.24, s32[8192]{0:T(1024)S(1)} %broadcast_clamp_fusion), kind=kCustom, calls=%fused_computation | custom fusion | bytes 4227072 | tf_op jit(solution)/shard_map/gather | solution.py:137
  29.8 0.0 copy-start.4
  29.8 2.8 %copy.15 = f32[64,64,128]{2,0,1:T(8,128)S(1)} copy(f32[64,64,128]{0,2,1:T(8,128)} %bitcast.25) | data formatting | bytes 4194304 | tf_op jit(solution)/shard_map/reshape | solution.py:137
  32.7 0.0 copy-done.4
  32.7 0.1 iota_compare_fusion
  32.8 1.6 broadcast_select_fusion
  34.4 0.0 copy-start.3
  34.4 0.0 copy-start.2
  34.4 13.9 %all-to-all-start = ((f32[64,64,128]{2,0,1:T(8,128)}), f32[64,64,128]{2,0,1:T(8,128)S(1)}, u32[]{:S(2)}, u32[]{:S(2)}) async-start(f32[64,64,128]{2,0,1:T(8,128)} %broadcast_select_fusion), calls=%async_computation | async-start | bytes 4194304 | tf_op jit(solution)/shard_map/all_to_all | solution.py:144
  48.3 0.0 copy-done.3
  48.4 51.1 %all-to-all-done = f32[64,64,128]{2,0,1:T(8,128)S(1)} async-done(((f32[64,64,128]{2,0,1:T(8,128)}), f32[64,64,128]{2,0,1:T(8,128)S(1)}, u32[]{:S(2)}, u32[]{:S(2)}) %all-to-all-start) | async-done | bytes 2097184 | tf_op jit(solution)/shard_map/all_to_all | solution.py:144
  99.4 0.0 copy-start
  99.4 1.3 copy-done
  100.8 0.0 copy-done.2
  100.8 1.8 bitcast_bitcast_fusion
  102.5 0.0 copy-start.1
  102.5 2.7 %copy.17 = f32[8192,64]{1,0:T(8,128)} copy(f32[8192,64]{0,1:T(8,128)S(1)} %bitcast_bitcast_fusion) | data formatting | bytes 4194304 | tf_op jit(solution)/shard_map/reshape | solution.py:147
  105.3 44.4 %scatter_custom_fusion = f32[64,1024]{0,1:T(8,128)S(1)} fusion(s32[8192]{0:T(1024)S(1)} %bitcast.34, f32[8192,64]{1,0:T(8,128)} %copy.17, f32[]{:T(128)} %constant.3.clone.1), kind=kCustom, calls=%fused_computation.6 | custom fusion | flops 524288 | bytes 262656 | tf_op jit(solution)/shard_map/scatter-add | solution.py:147
  149.7 0.2 copy.19
  149.9 0.0 copy-done.1
  149.9 0.7 bitcast_add_fusion.source_ref
  150.6 28.4 %sweep.1 = f32[64,8,128]{2,1,0:T(8,128)} custom-call(s32[8]{0:T(128)} %bitcast.35, f32[64,8,128]{2,1,0:T(8,128)} %bitcast_add_fusion.source_ref, f32[8,128,128]{2,1,0:T(8,128)} %bitcast.28, f32[8,128,128]{2,1,0:T(8,128)} %bitcast.29), custom_call_target="tpu_custom_call" | custom-call | tf_op jit(solution)/shard_map/sweep/pallas_call | solution.py:111
  179.0 1.7 copy.23
  (2 shorter events, 0.0 us)
Async XLA Ops:
  29.8 2.8 %copy-start.4 = (s32[1,1,64]{2,1,0:T(1,128)S(1)}, s32[1,1,64]{2,1,0:T(1,128)}, u32[]{:S(2)}) copy-start(s32[1,1,64]{2,1,0:T(1,128)} %param.13) | copy-start | bytes 772
  34.4 13.9 %copy-start.3 = (s32[1,1,64,128]{3,2,1,0:T(8,128)S(1)}, s32[1,1,64,128]{3,2,1,0:T(8,128)}, u32[]{:S(2)}) copy-start(s32[1,1,64,128]{3,2,1,0:T(8,128)} %param.14) | copy-start | bytes 98308
  34.4 66.4 %copy-start.2 = (f32[1,1,64,128]{3,2,1,0:T(8,128)S(1)}, f32[1,1,64,128]{3,2,1,0:T(8,128)}, u32[]{:S(2)}) copy-start(f32[1,1,64,128]{3,2,1,0:T(8,128)} %param.15) | copy-start | bytes 98308
  34.4 65.1 %all-to-all-start = ((f32[64,64,128]{2,0,1:T(8,128)}), f32[64,64,128]{2,0,1:T(8,128)S(1)}, u32[]{:S(2)}, u32[]{:S(2)}) async-start(f32[64,64,128]{2,0,1:T(8,128)} %broadcast_select_fusion), calls=%async_computation | async-start | bytes 4194304 | tf_op jit(solution)/shard_map/all_to_all | solution.py:144
  99.4 1.3 copy-start
  102.5 47.4 %copy-start.1 = (f32[1,1,64,8,128]{4,3,2,1,0:T(8,128)S(1)}, f32[1,1,64,8,128]{4,3,2,1,0:T(8,128)}, u32[]{:S(2)}) copy-start(f32[1,1,64,8,128]{4,3,2,1,0:T(8,128)} %param.8) | copy-start | bytes 786436

commit v2 on v1

v2 whole, which is shorter than its diff:
```python
import jax
import jax.numpy as jnp
from jax import lax
from jax.experimental import pallas as pl
from jax.experimental.pallas import tpu as pltpu
from jax.sharding import PartitionSpec as P

MESH = pl.DeviceIdType.MESH
E, NB, B = 64, 8, 128
CELLS = NB * B
N_FLOW = 8
NX, NZ, NC = 4, 8, 2
GROUP = NX * NC
SUBS = 4
WIDE = 256


def split(value):
    high = value.astype(jnp.bfloat16)
    low = (value - high.astype(jnp.float32)).astype(jnp.bfloat16)
    return high, low


def dot(left, right):
    return jnp.dot(left, right, preferred_element_type=jnp.float32)


def dot3(left, right):
    left_high, left_low = left
    right_high, right_low = right
    return dot(left_high, right_high) + dot(left_low, right_high) + dot(left_high, right_low)


def one_hot(row, first, iota_ref):
    shifted = row - first
    inside = (shifted >= 0.0) & (shifted < float(WIDE))
    place = jnp.where(inside, shifted, -1.0).astype(jnp.bfloat16)
    hit = jnp.broadcast_to(place, (WIDE, WIDE)) == iota_ref[...]
    return jnp.where(hit, jnp.bfloat16(1), jnp.bfloat16(0))


def step_kernel(feeders, counts, conc_ref, flux_ref, inverse_ref, send_ref, cells_ref, coef_ref, out_ref,
                held, lhs, iota_ref, send_rows, zmeta, recv_rows, xmeta, xrow, weighted,
                to_partner, from_partner, comb, relay, final,
                resp_high, resp_low, src, local, incoming, outlet,
                right_send, right_recv, left_send, left_recv,
                zm_send, zm_recv, xm_send, xm_recv,
                pair_send, pair_recv, relay_send, relay_recv, final_send, final_recv,
                flow_send, flow_recv):
    flow = lax.axis_index("flow")
    cross = lax.axis_index("cross")
    x = cross // (NZ * NC)
    z = lax.rem(cross // NC, NZ)
    c = lax.rem(cross, NC)

    def peer(px, pz, pc):
        return {"cross": (px * NZ + pz) * NC + pc}

    def near(dx=0, dz=0, dc=0):
        return peer(lax.rem(x + dx + NX, NX), lax.rem(z + dz + NZ, NZ), lax.rem(c + dc, NC))

    flow_right = {"flow": lax.rem(flow + 1, N_FLOW)}
    flow_left = {"flow": lax.rem(flow + N_FLOW - 1, N_FLOW)}
    group = [(dx, dc) for dx in range(NX) for dc in range(NC)]

    barrier = pltpu.get_barrier_semaphore()
    greeted = [near(dz=k) for k in range(1, NZ)] + [near(dx=dx, dc=dc) for dx, dc in group[1:]]
    greeted += [flow_right, flow_left]
    for other in greeted:
        pl.semaphore_signal(barrier, inc=1, device_id=other, device_id_type=MESH)

    for b in range(NB):
        held[0, b] = conc_ref[:, b, :]
    lane = lax.broadcasted_iota(jnp.int32, (1, B), 1)
    for pz in range(NZ):
        for g in range(GROUP):
            peer_id = (g // NC) * NZ * NC + pz * NC + g % NC
            row = send_ref[pl.ds(peer_id, 1), :]
            live = jnp.where(lane < counts[peer_id], row, -1)
            send_rows[pz, pl.ds(g, 1), :] = live.astype(jnp.float32)
    for g in range(GROUP):
        rows = pl.ds((g // NC) * NZ * NC + g % NC, NZ, stride=NC)
        recv_rows[g, pl.ds(0, NZ), :] = cells_ref[rows, :].astype(jnp.float32)
        recv_rows[g, pl.ds(NZ, NZ), :] = coef_ref[rows, :]
    iota_ref[...] = lax.broadcasted_iota(jnp.int32, (WIDE, WIDE), 0).astype(jnp.float32).astype(jnp.bfloat16)

    def right_copy(r, i):
        part = pl.ds(2 * i, 2)
        return pltpu.make_async_remote_copy(
            src_ref=held.at[r, part], dst_ref=held.at[r + 1, part],
            send_sem=right_send.at[r, i], recv_sem=right_recv.at[r, i],
            device_id=near(dz=1), device_id_type=MESH)

    def left_copy(r, i):
        part = pl.ds(2 * i, 2)
        return pltpu.make_async_remote_copy(
            src_ref=held.at[(NZ - r) % NZ, part], dst_ref=held.at[NZ - r - 1, part],
            send_sem=left_send.at[r, i], recv_sem=left_recv.at[r, i],
            device_id=near(dz=-1), device_id_type=MESH)

    def zmeta_copy(k):
        return pltpu.make_async_remote_copy(
            src_ref=send_rows.at[lax.rem(z + k, NZ)], dst_ref=zmeta.at[k],
            send_sem=zm_send.at[k], recv_sem=zm_recv.at[k],
            device_id=near(dz=k), device_id_type=MESH)

    def xmeta_copy(dx, dc):
        to_x, to_c = lax.rem(x + NX - dx, NX), lax.rem(c + dc, NC)
        return pltpu.make_async_remote_copy(
            src_ref=recv_rows.at[to_x * NC + to_c], dst_ref=xmeta.at[dx * NC + dc],
            send_sem=xm_send.at[dx * NC + dc], recv_sem=xm_recv.at[dx * NC + dc],
            device_id=peer(to_x, z, to_c), device_id_type=MESH)

    def pair_copy(dx):
        return pltpu.make_async_remote_copy(
            src_ref=to_partner.at[dx], dst_ref=from_partner.at[dx],
            send_sem=pair_send.at[dx], recv_sem=pair_recv.at[dx],
            device_id=near(dc=1), device_id_type=MESH)

    def relay_copy(side):
        return pltpu.make_async_remote_copy(
            src_ref=comb.at[2, pl.ds(4 * side, 4)], dst_ref=relay.at[side],
            send_sem=relay_send.at[side], recv_sem=relay_recv.at[side],
            device_id=near(dx=1 - 2 * side), device_id_type=MESH)

    def final_copy(side, half):
        part = pl.ds(4 * half, 4)
        return pltpu.make_async_remote_copy(
            src_ref=comb.at[1 + 2 * side, part], dst_ref=final.at[side, part],
            send_sem=final_send.at[side, half], recv_sem=final_recv.at[side, half],
            device_id=near(dx=1 - 2 * side), device_id_type=MESH)

    flow_copy = pltpu.make_async_remote_copy(
        src_ref=outlet, dst_ref=incoming, send_sem=flow_send, recv_sem=flow_recv,
        device_id=flow_right, device_id_type=MESH)

    def response_start():
        resp_high[0] = jnp.zeros((CELLS + B, B), jnp.bfloat16)
        resp_low[0] = jnp.zeros((CELLS + B, B), jnp.bfloat16)
        own = split(inverse_ref[0])
        first = split(dot3(split(flux_ref[0]), own))
        resp_high[0, pl.ds(CELLS, B), :] = first[0]
        resp_low[0, pl.ds(CELLS, B), :] = first[1]
        resp_high[0, pl.ds(0, B), :] = own[0]
        resp_low[0, pl.ds(0, B), :] = own[1]

    def response_step(j):
        feeder = feeders[j]
        own = split(inverse_ref[j])
        step = split(dot3(split(flux_ref[j]), own))
        rows = split(dot3((resp_high[feeder], resp_low[feeder]), step))
        resp_high[j] = rows[0]
        resp_low[j] = rows[1]
        spot = pl.ds(pl.multiple_of(j * B, B), B)
        resp_high[j, spot, :] = own[0]
        resp_low[j, spot, :] = own[1]

    def load_lhs(r, which):
        for b in range(NB):
            high, low = split(held[r, b])
            lhs[which, pl.ds(0, E), pl.ds(b * B, B)] = high
            lhs[which, pl.ds(E, E), pl.ds(b * B, B)] = low

    def pick(r, which, p):
        at = lax.rem(x + p, NX) * NC
        row = jnp.concatenate(
            [zmeta[r, pl.ds(at + lax.rem(c + dc, NC), 1), :] for dc in range(NC)], axis=1)
        zs = NZ + lax.rem(z + NZ - r, NZ)
        coef = jnp.concatenate(
            [xmeta[p * NC + dc, pl.ds(zs, 1), :] for dc in range(NC)], axis=1)
        choice = jnp.concatenate([one_hot(row, float(WIDE * q), iota_ref) for q in range(SUBS)], axis=0)
        both = dot(lhs[which], choice)
        value = (both[:E] + both[E:]) * coef
        high, low = split(value)
        for dc in range(NC):
            weighted[p * NC + dc, pl.ds(0, E), pl.ds(r * B, B)] = high[:, dc * B:(dc + 1) * B]
            weighted[p * NC + dc, pl.ds(E, E), pl.ds(r * B, B)] = low[:, dc * B:(dc + 1) * B]

    def deposit(d, put):
        def chunk(q, carry):
            first = (q * WIDE).astype(jnp.float32)
            landing = jnp.concatenate(
                [one_hot(xrow[d, :, i * WIDE:(i + 1) * WIDE], first, iota_ref) for i in range(SUBS)], axis=1)
            both = lax.dot_general(weighted[d], landing, (((1,), (1,)), ((), ())),
                                   preferred_element_type=jnp.float32)
            value = both[:E] + both[E:]
            put[2 * q] = value[:, :B]
            put[2 * q + 1] = value[:, B:]
            return carry
        lax.fori_loop(0, SUBS, chunk, 0)

    pl.semaphore_wait(barrier, len(greeted))
    for k in range(1, NZ):
        zmeta_copy(k).start()
    for dx, dc in group[1:]:
        xmeta_copy(dx, dc).start()
    for i in range(SUBS):
        right_copy(0, i).start()
        left_copy(0, i).start()

    zmeta[0] = send_rows[z]
    xmeta[0] = recv_rows[x * NC + c]
    response_start()
    lax.fori_loop(1, 4, lambda j, carry: (response_step(j), carry)[1], 0)
    load_lhs(0, 0)
    for dx, dc in group[1:]:
        xmeta_copy(dx, dc).wait_recv()
    for d in range(GROUP):
        for r in range(NZ):
            xrow[d, :, pl.ds(r * B, B)] = xmeta[d, pl.ds(lax.rem(z + NZ - r, NZ), 1), :]

    for r in range(1, 4):
        if r > 1:
            zmeta_copy(r - 1).wait_recv()
            zmeta_copy(NZ - r + 1).wait_recv()
            load_lhs(r - 1, 0)
            load_lhs(NZ - r + 1, 1)

        def ring(i, carry, r=r):
            right_copy(r - 1, i).wait_recv()
            if r < 3:
                right_copy(r, i).start()
            else:
                @pl.when(i < 2)
                def _():
                    right_copy(r, i).start()
            left_copy(r - 1, i).wait_recv()
            if r < 3:
                left_copy(r, i).start()
            else:
                @pl.when(i >= 2)
                def _():
                    left_copy(r, i).start()
            if r == 1:
                response_step(4 + i)
                pick(0, 0, i)
            else:
                pick(r - 1, 0, i)
                pick(NZ - r + 1, 1, i)
            return carry

        lax.fori_loop(0, SUBS, ring, 0)

    zmeta_copy(3).wait_recv()
    zmeta_copy(5).wait_recv()
    zmeta_copy(4).wait_recv()
    load_lhs(3, 0)
    load_lhs(5, 1)

    def late(p, carry):
        pick(3, 0, p)
        pick(5, 1, p)
        return carry

    lax.fori_loop(0, SUBS, late, 0)
    for i in range(2):
        right_copy(3, i).wait_recv()
        left_copy(3, i + 2).wait_recv()
    load_lhs(4, 0)
    lax.fori_loop(0, SUBS, lambda p, carry: (pick(4, 0, p), carry)[1], 0)

    def combine(dx):
        pair_copy(dx).wait_recv()
        comb[dx] = comb[dx] + from_partner[dx]

    deposit(2 * NC + 1, to_partner.at[2])
    pair_copy(2).start()
    deposit(2 * NC, comb.at[2])
    deposit(1 * NC + 1, to_partner.at[1])
    pair_copy(1).start()
    combine(2)
    relay_copy(0).start()
    relay_copy(1).start()
    deposit(1 * NC, comb.at[1])
    deposit(3 * NC + 1, to_partner.at[3])
    pair_copy(3).start()
    combine(1)
    final_copy(0, 1).start()
    deposit(3 * NC, comb.at[3])
    deposit(1, to_partner.at[0])
    pair_copy(0).start()
    combine(3)
    final_copy(1, 0).start()
    relay_copy(0).wait_recv()
    comb[1, pl.ds(0, 4)] = comb[1, pl.ds(0, 4)] + relay[0]
    final_copy(0, 0).start()
    relay_copy(1).wait_recv()
    comb[3, pl.ds(4, 4)] = comb[3, pl.ds(4, 4)] + relay[1]
    final_copy(1, 1).start()
    deposit(0, comb.at[0])
    combine(0)
    comb[0] = comb[0] + held[0]
    for side, half in ((0, 1), (1, 0), (0, 0), (1, 1)):
        final_copy(side, half).wait_recv()
    for b in range(NB):
        high, low = split(comb[0, b] + final[0, b] + final[1, b])
        src[pl.ds(0, E), pl.ds(b * B, B)] = high
        src[pl.ds(E, E), pl.ds(b * B, B)] = low

    def solve(j):
        both = dot(src[...], resp_high[j, pl.ds(0, CELLS), :])
        return both[:E] + both[E:] + dot(src[pl.ds(0, E), :], resp_low[j, pl.ds(0, CELLS), :])

    def entering(j, parts):
        return dot3(parts, (resp_high[j, pl.ds(CELLS, B), :], resp_low[j, pl.ds(CELLS, B), :]))

    last = solve(NB - 1)

    @pl.when(flow == 0)
    def _():
        outlet[...] = last
        flow_copy.start()
        incoming[...] = jnp.zeros_like(incoming)

    for j in range(NB - 1):
        local[j] = solve(j)

    @pl.when(flow > 0)
    def _():
        flow_copy.wait_recv()
        outlet[...] = last + entering(NB - 1, split(incoming[...]))

        @pl.when(flow < N_FLOW - 1)
        def _():
            flow_copy.start()

    out_ref[:, NB - 1, :] = outlet[...]
    parts = split(incoming[...])
    for j in range(NB - 1):
        out_ref[:, j, :] = local[j] + entering(j, parts)

    for k in range(1, NZ):
        zmeta_copy(k).wait_send()
    for dx, dc in group[1:]:
        xmeta_copy(dx, dc).wait_send()
    for r in range(3):
        for i in range(SUBS):
            right_copy(r, i).wait_send()
            left_copy(r, i).wait_send()
    for i in range(2):
        right_copy(3, i).wait_send()
        left_copy(3, i + 2).wait_send()
    for dx in range(NX):
        pair_copy(dx).wait_send()
    for side in range(2):
        relay_copy(side).wait_send()
        for half in range(2):
            final_copy(side, half).wait_send()

    @pl.when(flow < N_FLOW - 1)
    def _():
        flow_copy.wait_send()


def step(feeders, counts, conc, couplings, inverses, send_cells, recv_cells, recv_coef):
    vmem = pl.BlockSpec(memory_space=pltpu.VMEM)
    smem = pl.BlockSpec(memory_space=pltpu.SMEM)
    f32, bf16 = jnp.float32, jnp.bfloat16
    dma = pltpu.SemaphoreType.DMA
    return pl.pallas_call(
        step_kernel,
        out_shape=jax.ShapeDtypeStruct((E, NB, B), f32),
        in_specs=[smem, smem] + [vmem] * 6,
        out_specs=vmem,
        scratch_shapes=[
            pltpu.VMEM((NZ, NB, E, B), f32),
            pltpu.VMEM((2, 2 * E, CELLS), bf16),
            pltpu.VMEM((WIDE, WIDE), bf16),
            pltpu.VMEM((NZ, GROUP, B), f32),
            pltpu.VMEM((NZ, GROUP, B), f32),
            pltpu.VMEM((GROUP, 2 * NZ, B), f32),
            pltpu.VMEM((GROUP, 2 * NZ, B), f32),
            pltpu.VMEM((GROUP, 1, CELLS), f32),
            pltpu.VMEM((GROUP, 2 * E, CELLS), bf16),
            pltpu.VMEM((NX, NB, E, B), f32),
            pltpu.VMEM((NX, NB, E, B), f32),
            pltpu.VMEM((NX, NB, E, B), f32),
            pltpu.VMEM((2, 4, E, B), f32),
            pltpu.VMEM((2, NB, E, B), f32),
            pltpu.VMEM((NB, CELLS + B, B), bf16),
            pltpu.VMEM((NB, CELLS + B, B), bf16),
            pltpu.VMEM((2 * E, CELLS), bf16),
            pltpu.VMEM((NB, E, B), f32),
            pltpu.VMEM((E, B), f32),
            pltpu.VMEM((E, B), f32),
            dma((4, SUBS)), dma((4, SUBS)), dma((4, SUBS)), dma((4, SUBS)),
            dma((NZ,)), dma((NZ,)), dma((GROUP,)), dma((GROUP,)),
            dma((NX,)), dma((NX,)), dma((2,)), dma((2,)), dma((2, 2)), dma((2, 2)),
            dma, dma,
        ],
        compiler_params=pltpu.CompilerParams(collective_id=0, has_side_effects=True),
        name="transport_step",
    )(feeders, counts, conc, couplings, inverses, send_cells, recv_cells, recv_coef)


def on_device(conc_old, face_flux, block_inverse, upstream_block, send_cells, send_count, recv_cells, recv_coef):
    return step(
        upstream_block[0, 0], send_count[0, 0], conc_old[0, 0], face_flux[0, 0], block_inverse[0, 0],
        send_cells[0, 0], recv_cells[0, 0], recv_coef[0, 0])[None, None]


def solution(mesh):
    placed = (
        P("flow", "cross", None, None, None),
        P("flow", "cross", None, None, None),
        P("flow", "cross", None, None, None),
        P("flow", "cross", None),
        P("flow", "cross", None, None),
        P("flow", "cross", None),
        P("flow", "cross", None, None),
        P("flow", "cross", None, None),
    )
    return jax.shard_map(
        on_device,
        mesh=mesh,
        in_specs=placed,
        out_specs=P("flow", "cross", None, None, None),
        check_vma=False,
    )
```

time: 181 us -> 77.1 us (0.43)
  waiting for transfers between devices: 51.1 us -> 0 us
  other arithmetic: 49.5 us -> 0 us
  Pallas kernels: 28.4 us -> 75.2 us
  local copies, waits for them, and re-layouts: 37.8 us -> 1.67 us
  starting transfers between devices: 13.9 us -> 0 us
    all_to_all x1 -> x0, waiting for transfers between devices: 51.1 us -> none  [on_device(): lax.all_to_all(outgoing, 'cross', split_axis=1, concat_axis=1, tiled=True)]
    pallas_call x1, Pallas kernels: 28.4 us -> 75.2 us  [step(): pl.pallas_call(step_kernel, out_shape=jax.ShapeDtypeStruct((E, NB, B), f3...]
    scatter-add x1 -> x0, other arithmetic: 44.4 us -> none  [on_device(): lateral = empty.at[:, targets].add(weighted.reshape(arrived.shape[0], -1))]
    gather x1 -> x0, local copies, waits for them, and re-layouts: 27.8 us -> none  [on_device(): picked = flat_conc[:, send_index].reshape(members, n_cross, slot_count)]
    all_to_all x1 -> x0, starting transfers between devices: 13.9 us -> none  [on_device(): lax.all_to_all(outgoing, 'cross', split_axis=1, concat_axis=1, tiled=True)]
    reshape x3 -> x0, local copies, waits for them, and re-layouts: 5.74 us -> none  [the longest x1 2.84 us: on_device(): picked = flat_conc[:, send_index].reshape(members, n_cross, slot_count)]
    unnamed x12 -> x1, local copies, waits for them, and re-layouts: 4.16 us -> 1.67 us
    select_n x3 -> x0, other arithmetic: 2.45 us -> none  [the longest x1 1.62 us: on_device(): outgoing = jnp.where(live_slot[None], picked, 0.0)]
  transfers between devices with their start and end apart: 1 -> 0, of which waited for: 1 -> 0; matrix products, arithmetic and copies ran while one was open for 0% -> 0% of each run, Pallas kernels for 0% -> 0%
where the time goes in v2:
time: 77.1 us; the launch traced here: 76.9 us
  Pallas kernels  75.2 us (98%)
  local copies, waits for them, and re-layouts  1.67 us (2%)
    pallas_call x1, Pallas kernels, step(): pl.pallas_call(step_kernel, out_shape=jax.ShapeDtypeStruct((E, NB, B), f3...  75.2 us
    unnamed x1, local copies, waits for them, and re-layouts  1.67 us

profile of v2, /device:TPU:56, one launch (start us, length us, event | category | flops | bytes accessed | tf_op | source)
XLA Modules:
  0.0 76.9 jit_solution(4547273468718556185)
XLA Ops:
  0.0 75.2 %transport_step.1 = f32[64,8,128]{2,1,0:T(8,128)} custom-call(s32[8]{0:T(128)} %bitcast.16, s32[64]{0:T(128)} %bitcast.17, f32[64,8,128]{2,1,0:T(8,128)} %bitcast.12, f32[8,128,128]{2,1,0:T(8,128)} %bitcast.10, f32[8,128,128]{2,1,0:T(8,128)} %bitcast.11, s32[64,128]{1,0:T(8,128)} %bitcast.13, s32[64,128]{1,0:T(8,128)} %bitcast.14, f32[64,128]{1,0:T(8,128)} %bitcast.15), custom_call_target="tpu_custom_call" | custom-call | tf_op jit(solution)/shard_map/transport_step/pallas_call | solution.py:360
  75.2 1.7 %copy.10 = f32[1,1,64,8,128]{4,3,2,1,0:T(8,128)} copy(f32[1,1,64,8,128]{4,3,2,1,0:T(8,128)} %bitcast.9) | data formatting | bytes 524288

commit v3 on v2

v3 whole, which is shorter than its diff:
```python
import jax
import jax.numpy as jnp
from jax import lax
from jax.experimental import pallas as pl
from jax.experimental.pallas import tpu as pltpu
from jax.sharding import PartitionSpec as P

MESH = pl.DeviceIdType.MESH
E, NB, B = 64, 8, 128
CELLS = NB * B
N_FLOW = 8
NX, NZ, NC = 4, 8, 2
GROUP = NX * NC
SUBS = 4
WIDE = 256
ORDER = ((0, 1), (7, 2), (6, 3), (5, 4))
WHERE = {r: (t, half) for t, pair in enumerate(ORDER) for half, r in enumerate(pair)}


def split(value):
    high = value.astype(jnp.bfloat16)
    low = (value - high.astype(jnp.float32)).astype(jnp.bfloat16)
    return high, low


def dot(left, right):
    return jnp.dot(left, right, preferred_element_type=jnp.float32)


def dot3(left, right):
    left_high, left_low = left
    right_high, right_low = right
    return dot(left_high, right_high) + dot(left_low, right_high) + dot(left_high, right_low)


def one_hot(row, first, iota_ref):
    shifted = row - first
    inside = (shifted >= 0.0) & (shifted < float(WIDE))
    place = jnp.where(inside, shifted, -1.0).astype(jnp.bfloat16)
    hit = jnp.broadcast_to(place, (WIDE, WIDE)) == iota_ref[...]
    return jnp.where(hit, jnp.bfloat16(1), jnp.bfloat16(0))


def scaled_rows(matrix):
    top = jnp.maximum(jnp.max(matrix, axis=1, keepdims=True), 1e-30)
    column = jnp.broadcast_to(top, (B, B))
    return matrix / column, jnp.transpose(column)[0:1, :]


def step_kernel(feeders_in, counts_in, conc_in, flux_in, inverse_in, send_in, cells_in, coef_in,
                settled_ref, entered_ref,
                feeders, counts, conc_ref, flux_ref, inverse_ref, send_ref, cells_ref, coef_ref,
                held, lhs, iota_ref, send_rows, zmeta, recv_rows, xmeta, xrow, weighted,
                to_partner, from_partner, comb, relay, final,
                resp_high, resp_low, src, outlet, passing, above, passages,
                chain_high, chain_low, chain_scale, arriving,
                load_sem,
                right_send, right_recv, left_send, left_recv,
                zm_send, zm_recv, xm_send, xm_recv,
                pair_send, pair_recv, relay_send, relay_recv, final_send, final_recv,
                above_send, above_recv, pass_send, pass_recv):
    flow = lax.axis_index("flow")
    cross = lax.axis_index("cross")
    x = cross // (NZ * NC)
    z = lax.rem(cross // NC, NZ)
    c = lax.rem(cross, NC)

    def peer(px, pz, pc):
        return {"cross": (px * NZ + pz) * NC + pc}

    def near(dx=0, dz=0, dc=0):
        return peer(lax.rem(x + dx + NX, NX), lax.rem(z + dz + NZ, NZ), lax.rem(c + dc, NC))

    group = [(dx, dc) for dx in range(NX) for dc in range(NC)]

    barrier = pltpu.get_barrier_semaphore()
    greeted = [near(dz=k) for k in range(1, NZ)] + [near(dx=dx, dc=dc) for dx, dc in group[1:]]
    greeted += [{"flow": lax.rem(flow + k, N_FLOW)} for k in range(1, N_FLOW)]
    for other in greeted:
        pl.semaphore_signal(barrier, inc=1, device_id=other, device_id_type=MESH)

    loads = [pltpu.make_async_copy(a, b, load_sem.at[i]) for i, (a, b) in enumerate((
        (conc_in, conc_ref), (counts_in, counts), (send_in, send_ref), (cells_in, cells_ref),
        (coef_in, coef_ref), (feeders_in, feeders), (flux_in, flux_ref), (inverse_in, inverse_ref)))]
    for load in loads:
        load.start()
    iota_ref[...] = lax.broadcasted_iota(jnp.int32, (WIDE, WIDE), 0).astype(jnp.float32).astype(jnp.bfloat16)
    for k in range(1, N_FLOW):
        @pl.when(flow < k)
        def _(k=k):
            above[k - 1] = jnp.zeros((E, B), jnp.float32)
    for k in range(1, N_FLOW - 1):
        @pl.when(flow <= k)
        def _(k=k):
            passages[k - 1] = jnp.zeros((B, B), jnp.float32)
    loads[0].wait()
    for b in range(NB):
        held[0, b] = conc_ref[:, b, :]
    for load in loads[1:5]:
        load.wait()
    lane = lax.broadcasted_iota(jnp.int32, (1, B), 1)
    for pz in range(NZ):
        for g in range(GROUP):
            peer_id = (g // NC) * NZ * NC + pz * NC + g % NC
            row = send_ref[pl.ds(peer_id, 1), :]
            live = jnp.where(lane < counts[peer_id], row, -1)
            send_rows[pz, pl.ds(g, 1), :] = live.astype(jnp.float32)
    for g in range(GROUP):
        rows = pl.ds((g // NC) * NZ * NC + g % NC, NZ, stride=NC)
        recv_rows[g, pl.ds(0, NZ), :] = cells_ref[rows, :].astype(jnp.float32)
        recv_rows[g, pl.ds(NZ, NZ), :] = coef_ref[rows, :]

    def right_copy(r, i):
        part = pl.ds(2 * i, 2)
        return pltpu.make_async_remote_copy(
            src_ref=held.at[r, part], dst_ref=held.at[r + 1, part],
            send_sem=right_send.at[r, i], recv_sem=right_recv.at[r, i],
            device_id=near(dz=1), device_id_type=MESH)

    def left_copy(r, i):
        part = pl.ds(2 * i, 2)
        return pltpu.make_async_remote_copy(
            src_ref=held.at[(NZ - r) % NZ, part], dst_ref=held.at[NZ - r - 1, part],
            send_sem=left_send.at[r, i], recv_sem=left_recv.at[r, i],
            device_id=near(dz=-1), device_id_type=MESH)

    def zmeta_copy(k):
        return pltpu.make_async_remote_copy(
            src_ref=send_rows.at[lax.rem(z + k, NZ)], dst_ref=zmeta.at[k],
            send_sem=zm_send.at[k], recv_sem=zm_recv.at[k],
            device_id=near(dz=k), device_id_type=MESH)

    def xmeta_copy(dx, dc):
        to_x, to_c = lax.rem(x + NX - dx, NX), lax.rem(c + dc, NC)
        return pltpu.make_async_remote_copy(
            src_ref=recv_rows.at[to_x * NC + to_c], dst_ref=xmeta.at[dx * NC + dc],
            send_sem=xm_send.at[dx * NC + dc], recv_sem=xm_recv.at[dx * NC + dc],
            device_id=peer(to_x, z, to_c), device_id_type=MESH)

    def pair_copy(dx, q):
        part = pl.ds(2 * q, 2)
        return pltpu.make_async_remote_copy(
            src_ref=to_partner.at[dx, part], dst_ref=from_partner.at[dx, part],
            send_sem=pair_send.at[dx, q], recv_sem=pair_recv.at[dx, q],
            device_id=near(dc=1), device_id_type=MESH)

    def relay_copy(q):
        return pltpu.make_async_remote_copy(
            src_ref=comb.at[2, pl.ds(2 * q, 2)], dst_ref=relay.at[q],
            send_sem=relay_send.at[q], recv_sem=relay_recv.at[q],
            device_id=near(dx=1 if q < 2 else -1), device_id_type=MESH)

    def final_copy(side, q):
        part = pl.ds(2 * q, 2)
        return pltpu.make_async_remote_copy(
            src_ref=comb.at[1 + 2 * side, part], dst_ref=final.at[side, part],
            send_sem=final_send.at[side, q], recv_sem=final_recv.at[side, q],
            device_id=near(dx=1 - 2 * side), device_id_type=MESH)

    def above_copy(k):
        return pltpu.make_async_remote_copy(
            src_ref=outlet, dst_ref=above.at[k - 1],
            send_sem=above_send.at[k - 1], recv_sem=above_recv.at[k - 1],
            device_id={"flow": lax.rem(flow + k, N_FLOW)}, device_id_type=MESH)

    def pass_copy(k):
        return pltpu.make_async_remote_copy(
            src_ref=passing, dst_ref=passages.at[k - 1],
            send_sem=pass_send.at[k - 1], recv_sem=pass_recv.at[k - 1],
            device_id={"flow": lax.rem(flow + k, N_FLOW)}, device_id_type=MESH)

    def response_start():
        resp_high[0] = jnp.zeros((CELLS + B, B), jnp.bfloat16)
        resp_low[0] = jnp.zeros((CELLS + B, B), jnp.bfloat16)
        own = split(inverse_ref[0])
        first = split(dot3(split(flux_ref[0]), own))
        resp_high[0, pl.ds(CELLS, B), :] = first[0]
        resp_low[0, pl.ds(CELLS, B), :] = first[1]
        resp_high[0, pl.ds(0, B), :] = own[0]
        resp_low[0, pl.ds(0, B), :] = own[1]

    def response_step(j):
        feeder = feeders[j]
        own = split(inverse_ref[j])
        step = split(dot3(split(flux_ref[j]), own))
        rows = split(dot3((resp_high[feeder], resp_low[feeder]), step))
        resp_high[j] = rows[0]
        resp_low[j] = rows[1]
        spot = pl.ds(pl.multiple_of(j * B, B), B)
        resp_high[j, spot, :] = own[0]
        resp_low[j, spot, :] = own[1]

    def load_lhs(r, which):
        for b in range(NB):
            high, low = split(held[r, b])
            lhs[which, pl.ds(0, E), pl.ds(b * B, B)] = high
            lhs[which, pl.ds(E, E), pl.ds(b * B, B)] = low

    def pick(r, which, p):
        at = lax.rem(x + p, NX) * NC
        row = jnp.concatenate(
            [zmeta[r, pl.ds(at + lax.rem(c + dc, NC), 1), :] for dc in range(NC)], axis=1)
        zs = NZ + lax.rem(z + NZ - r, NZ)
        coef = jnp.concatenate(
            [xmeta[p * NC + dc, pl.ds(zs, 1), :] for dc in range(NC)], axis=1)
        choice = jnp.concatenate([one_hot(row, float(WIDE * q), iota_ref) for q in range(SUBS)], axis=0)
        both = dot(lhs[which], choice)
        value = (both[:E] + both[E:]) * coef
        high, low = split(value)
        t, half = WHERE[r]
        lanes = pl.ds(half * B, B)
        for dc in range(NC):
            weighted[p * NC + dc, t, pl.ds(0, E), lanes] = high[:, dc * B:(dc + 1) * B]
            weighted[p * NC + dc, t, pl.ds(E, E), lanes] = low[:, dc * B:(dc + 1) * B]

    def deposit(p, dc, t, q):
        put = to_partner if dc else comb
        landing = one_hot(xrow[p * NC + dc, t], float(WIDE * q), iota_ref)
        both = lax.dot_general(weighted[p * NC + dc, t], landing, (((1,), (1,)), ((), ())),
                               preferred_element_type=jnp.float32)
        value = both[:E] + both[E:]
        for i in range(2):
            piece = value[:, i * B:(i + 1) * B]
            put[p, 2 * q + i] = piece if t == 0 else put[p, 2 * q + i] + piece

    def deposit_all(p, t):
        for q in range(SUBS):
            for dc in range(NC):
                deposit(p, dc, t, q)

    pl.semaphore_wait(barrier, len(greeted))
    for k in range(1, NZ):
        zmeta_copy(k).start()
    for dx, dc in group[1:]:
        xmeta_copy(dx, dc).start()
    for i in range(SUBS):
        right_copy(0, i).start()
        left_copy(0, i).start()

    for load in loads[5:]:
        load.wait()
    zmeta[0] = send_rows[z]
    xmeta[0] = recv_rows[x * NC + c]
    response_start()
    lax.fori_loop(1, 4, lambda j, carry: (response_step(j), carry)[1], 0)
    load_lhs(0, 0)
    for dx, dc in group[1:]:
        xmeta_copy(dx, dc).wait_recv()
    for d in range(GROUP):
        for r in range(NZ):
            t, half = WHERE[r]
            xrow[d, t, :, pl.ds(half * B, B)] = xmeta[d, pl.ds(lax.rem(z + NZ - r, NZ), 1), :]

    for r in range(1, 4):
        if r > 1:
            zmeta_copy(r - 1).wait_recv()
            zmeta_copy(NZ - r + 1).wait_recv()
            load_lhs(r - 1, 0)
            load_lhs(NZ - r + 1, 1)

        def ring(i, carry, r=r):
            right_copy(r - 1, i).wait_recv()
            if r < 3:
                right_copy(r, i).start()
            else:
                @pl.when(i < 2)
                def _():
                    right_copy(r, i).start()
            left_copy(r - 1, i).wait_recv()
            if r < 3:
                left_copy(r, i).start()
            else:
                @pl.when(i >= 2)
                def _():
                    left_copy(r, i).start()
            if r == 1:
                response_step(4 + i)
                pick(0, 0, i)
            else:
                pick(r - 1, 0, i)
                pick(NZ - r + 1, 1, i)
                deposit_all(i, r - 2)
            return carry

        lax.fori_loop(0, SUBS, ring, 0)
        if r == 1:
            passing[...] = (resp_high[NB - 1, pl.ds(CELLS, B), :].astype(jnp.float32)
                            + resp_low[NB - 1, pl.ds(CELLS, B), :].astype(jnp.float32))
            for k in range(1, N_FLOW - 1):
                @pl.when((flow >= 1) & (flow + k < N_FLOW))
                def _(k=k):
                    pass_copy(k).start()

    zmeta_copy(3).wait_recv()
    zmeta_copy(5).wait_recv()
    zmeta_copy(4).wait_recv()
    load_lhs(3, 0)
    load_lhs(5, 1)

    def late(p, carry):
        pick(3, 0, p)
        pick(5, 1, p)
        deposit_all(p, 2)
        return carry

    lax.fori_loop(0, SUBS, late, 0)
    for i in range(2):
        right_copy(3, i).wait_recv()
        left_copy(3, i + 2).wait_recv()
    load_lhs(4, 0)

    def finish(p, q):
        deposit(p, 1, 3, q)
        pair_copy(p, q).start()
        deposit(p, 0, 3, q)

    def combine(p, q):
        pair_copy(p, q).wait_recv()
        part = pl.ds(2 * q, 2)
        comb[p, part] = comb[p, part] + from_partner[p, part]

    pick(4, 0, 2)
    for q in range(SUBS):
        finish(2, q)
    pick(4, 0, 1)
    pick(4, 0, 3)
    for q in (0, 2, 1, 3):
        combine(2, q)
        relay_copy(q).start()
    early = ((0, 2), (1, 0), (0, 3), (1, 1))
    later = ((0, 0), (1, 2), (0, 1), (1, 3))
    for side, q in early:
        finish(1 + 2 * side, q)
    for side, q in early:
        combine(1 + 2 * side, q)
        final_copy(side, q).start()
    for side, q in later:
        finish(1 + 2 * side, q)
    for side, q in later:
        combine(1 + 2 * side, q)
    pick(4, 0, 0)
    for q in range(SUBS):
        finish(0, q)
    for side, q in later:
        relay_copy(q).wait_recv()
        part = pl.ds(2 * q, 2)
        comb[1 + 2 * side, part] = comb[1 + 2 * side, part] + relay[q]
        final_copy(side, q).start()
    for q in range(SUBS):
        combine(0, q)
    comb[0] = comb[0] + held[0]

    for k in range(1, N_FLOW - 1):
        @pl.when(flow > k)
        def _(k=k):
            pass_copy(k).wait_recv()
    link = [split(passages[k]) for k in range(N_FLOW - 2)]
    two, four, six = (dot3(link[2 * i + 1], link[2 * i]) for i in range(3))
    two_parts, four_parts = split(two), split(four)
    whole_five, scale_five = scaled_rows(passages[4])
    whole_six, scale_six = scaled_rows(six)
    upper = dot3(split(jnp.concatenate([whole_five, whole_six], axis=0)), four_parts)
    whole_three, scale_three = scaled_rows(passages[2])
    whole_four, scale_four = scaled_rows(four)
    upper_five, more_five = scaled_rows(upper[:B])
    upper_six, more_six = scaled_rows(upper[B:])
    longer = dot3(split(jnp.concatenate([whole_three, whole_four, upper_five, upper_six], axis=0)), two_parts)
    for k, matrix in enumerate((link[0], two_parts)):
        chain_high[pl.ds(k * B, B), :] = matrix[0]
        chain_low[pl.ds(k * B, B), :] = matrix[1]
    longer_parts = split(longer)
    chain_high[pl.ds(2 * B, 4 * B), :] = longer_parts[0]
    chain_low[pl.ds(2 * B, 4 * B), :] = longer_parts[1]
    ones = jnp.ones((1, B), jnp.float32)
    for k, (first, second) in enumerate((
            (ones, ones), (ones, ones), (scale_three, ones), (scale_four, ones),
            (scale_five, more_five), (scale_six, more_six))):
        chain_scale[k, pl.ds(0, 1), :] = first
        chain_scale[k, pl.ds(1, 1), :] = second

    for side, q in early:
        final_copy(side, q).wait_recv()
        part = pl.ds(2 * q, 2)
        comb[0, part] = comb[0, part] + final[side, part]
    for side, q in later:
        final_copy(side, q).wait_recv()
        for b in (2 * q, 2 * q + 1):
            high, low = split(comb[0, b] + final[side, b])
            src[pl.ds(0, E), pl.ds(b * B, B)] = high
            src[pl.ds(E, E), pl.ds(b * B, B)] = low

    def solve(j):
        both = dot(src[...], resp_high[j, pl.ds(0, CELLS), :])
        return both[:E] + both[E:] + dot(src[pl.ds(0, E), :], resp_low[j, pl.ds(0, CELLS), :])

    outlet[...] = solve(NB - 1)
    for k in (4, 3, 5, 2, 6, 1, 7):
        @pl.when(flow + k < N_FLOW)
        def _(k=k):
            above_copy(k).start()
    settled_ref[:, NB - 1, :] = outlet[...]
    for j in range(NB - 1):
        settled_ref[:, j, :] = solve(j)

    for k in (7, 6, 5, 4, 3, 2, 1):
        @pl.when(flow >= k)
        def _(k=k):
            above_copy(k).wait_recv()
        if k > 1:
            high, low = split(above[k - 1] * chain_scale[k - 2, pl.ds(0, 1), :] * chain_scale[k - 2, pl.ds(1, 1), :])
            arriving[pl.ds(0, E), pl.ds((k - 2) * B, B)] = high
            arriving[pl.ds(E, E), pl.ds((k - 2) * B, B)] = low
    both = dot(arriving[...], chain_high[...])
    inflow = above[0] + both[:E] + both[E:] + dot(arriving[pl.ds(0, E), :], chain_low[...])
    parts = split(inflow)
    for j in range(NB):
        entered_ref[:, j, :] = dot3(parts, (resp_high[j, pl.ds(CELLS, B), :], resp_low[j, pl.ds(CELLS, B), :]))

    for k in range(1, NZ):
        zmeta_copy(k).wait_send()
    for dx, dc in group[1:]:
        xmeta_copy(dx, dc).wait_send()
    for r in range(3):
        for i in range(SUBS):
            right_copy(r, i).wait_send()
            left_copy(r, i).wait_send()
    for i in range(2):
        right_copy(3, i).wait_send()
        left_copy(3, i + 2).wait_send()
    for q in range(SUBS):
        for dx in range(NX):
            pair_copy(dx, q).wait_send()
        relay_copy(q).wait_send()
        for side in range(2):
            final_copy(side, q).wait_send()
    for k in range(1, N_FLOW):
        @pl.when(flow + k < N_FLOW)
        def _(k=k):
            above_copy(k).wait_send()
    for k in range(1, N_FLOW - 1):
        @pl.when((flow >= 1) & (flow + k < N_FLOW))
        def _(k=k):
            pass_copy(k).wait_send()


def step(feeders, counts, conc, couplings, inverses, send_cells, recv_cells, recv_coef):
    vmem = pl.BlockSpec(memory_space=pltpu.VMEM)
    f32, bf16, i32 = jnp.float32, jnp.bfloat16, jnp.int32
    dma = pltpu.SemaphoreType.DMA
    settled, entered = pl.pallas_call(
        step_kernel,
        out_shape=[jax.ShapeDtypeStruct((E, NB, B), f32)] * 2,
        in_specs=[pl.BlockSpec(memory_space=pl.ANY)] * 8,
        out_specs=[vmem, vmem],
        scratch_shapes=[
            pltpu.SMEM((NB,), i32),
            pltpu.SMEM((NZ * GROUP,), i32),
            pltpu.VMEM((E, NB, B), f32),
            pltpu.VMEM((NB, B, B), f32),
            pltpu.VMEM((NB, B, B), f32),
            pltpu.VMEM((NZ * GROUP, B), i32),
            pltpu.VMEM((NZ * GROUP, B), i32),
            pltpu.VMEM((NZ * GROUP, B), f32),
            pltpu.VMEM((NZ, NB, E, B), f32),
            pltpu.VMEM((2, 2 * E, CELLS), bf16),
            pltpu.VMEM((WIDE, WIDE), bf16),
            pltpu.VMEM((NZ, GROUP, B), f32),
            pltpu.VMEM((NZ, GROUP, B), f32),
            pltpu.VMEM((GROUP, 2 * NZ, B), f32),
            pltpu.VMEM((GROUP, 2 * NZ, B), f32),
            pltpu.VMEM((GROUP, SUBS, 1, WIDE), f32),
            pltpu.VMEM((GROUP, SUBS, 2 * E, WIDE), bf16),
            pltpu.VMEM((NX, NB, E, B), f32),
            pltpu.VMEM((NX, NB, E, B), f32),
            pltpu.VMEM((NX, NB, E, B), f32),
            pltpu.VMEM((SUBS, 2, E, B), f32),
            pltpu.VMEM((2, NB, E, B), f32),
            pltpu.VMEM((NB, CELLS + B, B), bf16),
            pltpu.VMEM((NB, CELLS + B, B), bf16),
            pltpu.VMEM((2 * E, CELLS), bf16),
            pltpu.VMEM((E, B), f32),
            pltpu.VMEM((B, B), f32),
            pltpu.VMEM((N_FLOW - 1, E, B), f32),
            pltpu.VMEM((N_FLOW - 2, B, B), f32),
            pltpu.VMEM(((N_FLOW - 2) * B, B), bf16),
            pltpu.VMEM(((N_FLOW - 2) * B, B), bf16),
            pltpu.VMEM((N_FLOW - 2, 8, B), f32),
            pltpu.VMEM((2 * E, (N_FLOW - 2) * B), bf16),
            dma((8,)),
            dma((4, SUBS)), dma((4, SUBS)), dma((4, SUBS)), dma((4, SUBS)),
            dma((NZ,)), dma((NZ,)), dma((GROUP,)), dma((GROUP,)),
            dma((NX, SUBS)), dma((NX, SUBS)), dma((SUBS,)), dma((SUBS,)), dma((2, SUBS)), dma((2, SUBS)),
            dma((N_FLOW - 1,)), dma((N_FLOW - 1,)), dma((N_FLOW - 2,)), dma((N_FLOW - 2,)),
        ],
        compiler_params=pltpu.CompilerParams(collective_id=0, has_side_effects=True),
        name="transport_step",
    )(feeders, counts, conc, couplings, inverses, send_cells, recv_cells, recv_coef)
    return settled + entered


def on_device(conc_old, face_flux, block_inverse, upstream_block, send_cells, send_count, recv_cells, recv_coef):
    return step(
        upstream_block[0, 0], send_count[0, 0], conc_old[0, 0], face_flux[0, 0], block_inverse[0, 0],
        send_cells[0, 0], recv_cells[0, 0], recv_coef[0, 0])[None, None]


def solution(mesh):
    placed = (
        P("flow", "cross", None, None, None),
        P("flow", "cross", None, None, None),
        P("flow", "cross", None, None, None),
        P("flow", "cross", None),
        P("flow", "cross", None, None),
        P("flow", "cross", None),
        P("flow", "cross", None, None),
        P("flow", "cross", None, None),
    )
    return jax.shard_map(
        on_device,
        mesh=mesh,
        in_specs=placed,
        out_specs=P("flow", "cross", None, None, None),
        check_vma=False,
    )
```

time: 77.1 us -> 64 us (0.83)
  Pallas kernels: 75.2 us -> 62 us
  other arithmetic: 0 us -> 1.76 us
  local copies, waits for them, and re-layouts: 1.67 us -> 0 us
    pallas_call x1, Pallas kernels: 75.2 us -> 62 us  [step(): pl.pallas_call(step_kernel, out_shape=[jax.ShapeDtypeStruct((E, NB, B), f...]
    broadcast_in_dim x0 -> x1, other arithmetic: none -> 1.76 us  [on_device(): step(upstream_block[0, 0], send_count[0, 0], conc_old[0, 0], face_flux[0,...]
    unnamed x1 -> x0, local copies, waits for them, and re-layouts: 1.67 us -> none
where the time goes in v3:
time: 64 us; the launch traced here: 63.8 us
  Pallas kernels  62 us (97%)
  other arithmetic  1.76 us (3%)
    pallas_call x1, Pallas kernels, step(): pl.pallas_call(step_kernel, out_shape=[jax.ShapeDtypeStruct((E, NB, B), f...  62 us
    broadcast_in_dim x1, other arithmetic, on_device(): step(upstream_block[0, 0], send_count[0, 0], conc_old[0, 0], face_flux[0,...  1.76 us

profile of v3, /device:TPU:56, one launch (start us, length us, event | category | flops | bytes accessed | tf_op | source)
XLA Modules:
  0.0 63.8 jit_solution(5438471982943782041)
XLA Ops:
  0.0 62.0 %transport_step.1 = (f32[64,8,128]{2,1,0:T(8,128)}, f32[64,8,128]{2,1,0:T(8,128)}) custom-call(s32[8]{0:T(128)} %bitcast.16, s32[64]{0:T(128)} %bitcast.17, f32[64,8,128]{2,1,0:T(8,128)} %bitcast.12, f32[8,128,128]{2,1,0:T(8,128)} %bitcast.10, f32[8,128,128]{2,1,0:T(8,128)} %bitcast.11, s32[64,128]{1,0:T(8,128)} %bitcast.13, s32[64,128]{1,0:T(8,128)} %bitcast.14, ...), custom_call_target="tpu_custom_call" | custom-call | tf_op jit(solution)/shard_map/transport_step/pallas_call | solution.py:450
  62.0 1.8 %add_bitcast_fusion = f32[1,1,64,8,128]{4,3,2,1,0:T(8,128)} fusion(f32[64,8,128]{2,1,0:T(8,128)} %get-tuple-element.7, f32[64,8,128]{2,1,0:T(8,128)} %get-tuple-element.8), kind=kLoop, calls=%fused_computation | loop fusion | flops 65536 | bytes 786432 | tf_op jit(solution)/shard_map/broadcast_in_dim | solution.py:502

commit v4 on v3

--- a/solution.py
+++ b/solution.py
@@ -27,10 +27,20 @@
     return jnp.dot(left, right, preferred_element_type=jnp.float32)
 
 
-def dot3(left, right):
-    left_high, left_low = left
-    right_high, right_low = right
-    return dot(left_high, right_high) + dot(left_low, right_high) + dot(left_high, right_low)
+def beside(value):
+    return jnp.concatenate(split(value), axis=1)
+
+
+def product(left, right):
+    high, low = split(right)
+    whole = jnp.concatenate([jnp.concatenate([high, low], axis=1),
+                             jnp.concatenate([high, jnp.zeros_like(low)], axis=1)], axis=0)
+    both = dot(left, whole)
+    return both[:, :B] + both[:, B:]
+
+
+def corners(both):
+    return both[:E, :B] + both[E:, :B] + both[:E, B:]
 
 
 def one_hot(row, first, iota_ref):
@@ -50,15 +60,15 @@
 def step_kernel(feeders_in, counts_in, conc_in, flux_in, inverse_in, send_in, cells_in, coef_in,
                 settled_ref, entered_ref,
                 feeders, counts, conc_ref, flux_ref, inverse_ref, send_ref, cells_ref, coef_ref,
-                held, lhs, iota_ref, send_rows, zmeta, recv_rows, xmeta, xrow, weighted,
+                held, lhs, iota_ref, send_rows, lists, recv_rows, xmeta, xrow, weighted,
                 to_partner, from_partner, comb, relay, final,
-                resp_high, resp_low, src, outlet, passing, above, passages,
-                chain_high, chain_low, chain_scale, arriving,
+                resp, src, outlet, passing, above, passages,
+                chain, chain_scale, arriving,
                 load_sem,
                 right_send, right_recv, left_send, left_recv,
-                zm_send, zm_recv, xm_send, xm_recv,
+                list_send, list_recv, xm_send, xm_recv,
                 pair_send, pair_recv, relay_send, relay_recv, final_send, final_recv,
-                above_send, above_recv, pass_send, pass_recv):
+                above_send, above_recv, pass_send, pass_recv, rounds):
     flow = lax.axis_index("flow")
     cross = lax.axis_index("cross")
     x = cross // (NZ * NC)
@@ -74,8 +84,8 @@
     group = [(dx, dc) for dx in range(NX) for dc in range(NC)]
 
     barrier = pltpu.get_barrier_semaphore()
-    greeted = [near(dz=k) for k in range(1, NZ)] + [near(dx=dx, dc=dc) for dx, dc in group[1:]]
-    greeted += [{"flow": lax.rem(flow + k, N_FLOW)} for k in range(1, N_FLOW)]
+    flow_near = [{"flow": lax.rem(flow + k, N_FLOW)} for k in (1, N_FLOW - 1)]
+    greeted = [near(dz=1), near(dz=-1)] + [near(dx=dx, dc=dc) for dx, dc in group[1:]] + flow_near
     for other in greeted:
         pl.semaphore_signal(barrier, inc=1, device_id=other, device_id_type=MESH)
 
@@ -105,6 +115,10 @@
             row = send_ref[pl.ds(peer_id, 1), :]
             live = jnp.where(lane < counts[peer_id], row, -1)
             send_rows[pz, pl.ds(g, 1), :] = live.astype(jnp.float32)
+    for k in range(SUBS):
+        lists[0, 0, k] = send_rows[lax.rem(z + k + 1, NZ)]
+    for k in range(SUBS - 1):
+        lists[1, 0, k] = send_rows[lax.rem(z + NZ - k - 1, NZ)]
     for g in range(GROUP):
         rows = pl.ds((g // NC) * NZ * NC + g % NC, NZ, stride=NC)
         recv_rows[g, pl.ds(0, NZ), :] = cells_ref[rows, :].astype(jnp.float32)
@@ -124,11 +138,17 @@
             send_sem=left_send.at[r, i], recv_sem=left_recv.at[r, i],
             device_id=near(dz=-1), device_id_type=MESH)
 
-    def zmeta_copy(k):
-        return pltpu.make_async_remote_copy(
-            src_ref=send_rows.at[lax.rem(z + k, NZ)], dst_ref=zmeta.at[k],
-            send_sem=zm_send.at[k], recv_sem=zm_recv.at[k],
-            device_id=near(dz=k), device_id_type=MESH)
+    def list_copy(side, r):
+        far = (SUBS, SUBS - 1)[side]
+        part = pl.ds(r, far - r)
+        return pltpu.make_async_remote_copy(
+            src_ref=lists.at[side, r, part], dst_ref=lists.at[side, r + 1, part],
+            send_sem=list_send.at[side, r], recv_sem=list_recv.at[side, r],
+            device_id=near(dz=1 - 2 * side), device_id_type=MESH)
+
+    def tell(n):
+        for other in flow_near:
+            pl.semaphore_signal(rounds.at[n], inc=1, device_id=other, device_id_type=MESH)
 
     def xmeta_copy(dx, dc):
         to_x, to_c = lax.rem(x + NX - dx, NX), lax.rem(c + dc, NC)
@@ -170,25 +190,15 @@
             device_id={"flow": lax.rem(flow + k, N_FLOW)}, device_id_type=MESH)
 
     def response_start():
-        resp_high[0] = jnp.zeros((CELLS + B, B), jnp.bfloat16)
-        resp_low[0] = jnp.zeros((CELLS + B, B), jnp.bfloat16)
-        own = split(inverse_ref[0])
-        first = split(dot3(split(flux_ref[0]), own))
-        resp_high[0, pl.ds(CELLS, B), :] = first[0]
-        resp_low[0, pl.ds(CELLS, B), :] = first[1]
-        resp_high[0, pl.ds(0, B), :] = own[0]
-        resp_low[0, pl.ds(0, B), :] = own[1]
+        resp[0] = jnp.zeros((CELLS + B, 2 * B), jnp.bfloat16)
+        resp[0, pl.ds(CELLS, B), :] = beside(product(beside(flux_ref[0]), inverse_ref[0]))
+        resp[0, pl.ds(0, B), :] = beside(inverse_ref[0])
 
     def response_step(j):
-        feeder = feeders[j]
-        own = split(inverse_ref[j])
-        step = split(dot3(split(flux_ref[j]), own))
-        rows = split(dot3((resp_high[feeder], resp_low[feeder]), step))
-        resp_high[j] = rows[0]
-        resp_low[j] = rows[1]
-        spot = pl.ds(pl.multiple_of(j * B, B), B)
-        resp_high[j, spot, :] = own[0]
-        resp_low[j, spot, :] = own[1]
+        inverse = inverse_ref[j]
+        step = product(beside(flux_ref[j]), inverse)
+        resp[j] = beside(product(resp[feeders[j]], step))
+        resp[j, pl.ds(pl.multiple_of(j * B, B), B), :] = beside(inverse)
 
     def load_lhs(r, which):
         for b in range(NB):
@@ -198,8 +208,14 @@
 
     def pick(r, which, p):
         at = lax.rem(x + p, NX) * NC
+        if r == 0:
+            asked = send_rows.at[z]
+        elif r <= SUBS:
+            asked = lists.at[0, r, r - 1]
+        else:
+            asked = lists.at[1, NZ - r, NZ - r - 1]
         row = jnp.concatenate(
-            [zmeta[r, pl.ds(at + lax.rem(c + dc, NC), 1), :] for dc in range(NC)], axis=1)
+            [asked[pl.ds(at + lax.rem(c + dc, NC), 1), :] for dc in range(NC)], axis=1)
         zs = NZ + lax.rem(z + NZ - r, NZ)
         coef = jnp.concatenate(
             [xmeta[p * NC + dc, pl.ds(zs, 1), :] for dc in range(NC)], axis=1)
@@ -229,20 +245,19 @@
                 deposit(p, dc, t, q)
 
     pl.semaphore_wait(barrier, len(greeted))
-    for k in range(1, NZ):
-        zmeta_copy(k).start()
-    for dx, dc in group[1:]:
-        xmeta_copy(dx, dc).start()
     for i in range(SUBS):
         right_copy(0, i).start()
         left_copy(0, i).start()
-
+        if i == 0:
+            list_copy(0, 0).start()
+            list_copy(1, 0).start()
+            for dx, dc in group[1:]:
+                xmeta_copy(dx, dc).start()
+    tell(0)
     for load in loads[5:]:
         load.wait()
-    zmeta[0] = send_rows[z]
     xmeta[0] = recv_rows[x * NC + c]
     response_start()
-    lax.fori_loop(1, 4, lambda j, carry: (response_step(j), carry)[1], 0)
     load_lhs(0, 0)
     for dx, dc in group[1:]:
         xmeta_copy(dx, dc).wait_recv()
@@ -251,10 +266,15 @@
             t, half = WHERE[r]
             xrow[d, t, :, pl.ds(half * B, B)] = xmeta[d, pl.ds(lax.rem(z + NZ - r, NZ), 1), :]
 
+    pl.semaphore_wait(rounds.at[0], 2)
+    tell(1)
+
     for r in range(1, 4):
+        for side in range(2):
+            list_copy(side, r - 1).wait_recv()
+            if r < (SUBS, SUBS - 1)[side]:
+                list_copy(side, r).start()
         if r > 1:
-            zmeta_copy(r - 1).wait_recv()
-            zmeta_copy(NZ - r + 1).wait_recv()
             load_lhs(r - 1, 0)
             load_lhs(NZ - r + 1, 1)
 
@@ -274,7 +294,11 @@
                 def _():
                     left_copy(r, i).start()
             if r == 1:
-                response_step(4 + i)
+                response_step(2 * i + 1)
+
+                @pl.when(i < SUBS - 1)
+                def _():
+                    response_step(2 * i + 2)
                 pick(0, 0, i)
             else:
                 pick(r - 1, 0, i)
@@ -284,16 +308,18 @@
 
         lax.fori_loop(0, SUBS, ring, 0)
         if r == 1:
-            passing[...] = (resp_high[NB - 1, pl.ds(CELLS, B), :].astype(jnp.float32)
-                            + resp_low[NB - 1, pl.ds(CELLS, B), :].astype(jnp.float32))
+            passing[...] = (resp[NB - 1, pl.ds(CELLS, B), pl.ds(0, B)].astype(jnp.float32)
+                            + resp[NB - 1, pl.ds(CELLS, B), pl.ds(B, B)].astype(jnp.float32))
+            pl.semaphore_wait(rounds.at[1], 2)
+            tell(2)
+        if r == 2:
+            pl.semaphore_wait(rounds.at[2], 2)
             for k in range(1, N_FLOW - 1):
                 @pl.when((flow >= 1) & (flow + k < N_FLOW))
                 def _(k=k):
                     pass_copy(k).start()
 
-    zmeta_copy(3).wait_recv()
-    zmeta_copy(5).wait_recv()
-    zmeta_copy(4).wait_recv()
+    list_copy(0, 3).wait_recv()
     load_lhs(3, 0)
     load_lhs(5, 1)
 
@@ -354,23 +380,18 @@
         @pl.when(flow > k)
         def _(k=k):
             pass_copy(k).wait_recv()
-    link = [split(passages[k]) for k in range(N_FLOW - 2)]
-    two, four, six = (dot3(link[2 * i + 1], link[2 * i]) for i in range(3))
-    two_parts, four_parts = split(two), split(four)
+    two, four, six = (product(beside(passages[2 * i + 1]), passages[2 * i]) for i in range(3))
     whole_five, scale_five = scaled_rows(passages[4])
     whole_six, scale_six = scaled_rows(six)
-    upper = dot3(split(jnp.concatenate([whole_five, whole_six], axis=0)), four_parts)
+    upper = product(beside(jnp.concatenate([whole_five, whole_six], axis=0)), four)
     whole_three, scale_three = scaled_rows(passages[2])
     whole_four, scale_four = scaled_rows(four)
     upper_five, more_five = scaled_rows(upper[:B])
     upper_six, more_six = scaled_rows(upper[B:])
-    longer = dot3(split(jnp.concatenate([whole_three, whole_four, upper_five, upper_six], axis=0)), two_parts)
-    for k, matrix in enumerate((link[0], two_parts)):
-        chain_high[pl.ds(k * B, B), :] = matrix[0]
-        chain_low[pl.ds(k * B, B), :] = matrix[1]
-    longer_parts = split(longer)
-    chain_high[pl.ds(2 * B, 4 * B), :] = longer_parts[0]
-    chain_low[pl.ds(2 * B, 4 * B), :] = longer_parts[1]
+    longer = product(beside(jnp.concatenate([whole_three, whole_four, upper_five, upper_six], axis=0)), two)
+    chain[pl.ds(0, B), :] = beside(passages[0])
+    chain[pl.ds(B, B), :] = beside(two)
+    chain[pl.ds(2 * B, 4 * B), :] = beside(longer)
     ones = jnp.ones((1, B), jnp.float32)
     for k, (first, second) in enumerate((
             (ones, ones), (ones, ones), (scale_three, ones), (scale_four, ones),
@@ -390,8 +411,7 @@
             src[pl.ds(E, E), pl.ds(b * B, B)] = low
 
     def solve(j):
-        both = dot(src[...], resp_high[j, pl.ds(0, CELLS), :])
-        return both[:E] + both[E:] + dot(src[pl.ds(0, E), :], resp_low[j, pl.ds(0, CELLS), :])
+        return corners(dot(src[...], resp[j, pl.ds(0, CELLS), :]))
 
     outlet[...] = solve(NB - 1)
     for k in (4, 3, 5, 2, 6, 1, 7):
@@ -410,14 +430,14 @@
             high, low = split(above[k - 1] * chain_scale[k - 2, pl.ds(0, 1), :] * chain_scale[k - 2, pl.ds(1, 1), :])
             arriving[pl.ds(0, E), pl.ds((k - 2) * B, B)] = high
             arriving[pl.ds(E, E), pl.ds((k - 2) * B, B)] = low
-    both = dot(arriving[...], chain_high[...])
-    inflow = above[0] + both[:E] + both[E:] + dot(arriving[pl.ds(0, E), :], chain_low[...])
-    parts = split(inflow)
+    inflow = above[0] + corners(dot(arriving[...], chain[...]))
+    parts = jnp.concatenate(split(inflow), axis=0)
     for j in range(NB):
-        entered_ref[:, j, :] = dot3(parts, (resp_high[j, pl.ds(CELLS, B), :], resp_low[j, pl.ds(CELLS, B), :]))
-
-    for k in range(1, NZ):
-        zmeta_copy(k).wait_send()
+        entered_ref[:, j, :] = corners(dot(parts, resp[j, pl.ds(CELLS, B), :]))
+
+    for side in range(2):
+        for r in range((SUBS, SUBS - 1)[side]):
+            list_copy(side, r).wait_send()
     for dx, dc in group[1:]:
         xmeta_copy(dx, dc).wait_send()
     for r in range(3):
@@ -465,7 +485,7 @@
             pltpu.VMEM((2, 2 * E, CELLS), bf16),
             pltpu.VMEM((WIDE, WIDE), bf16),
             pltpu.VMEM((NZ, GROUP, B), f32),
-            pltpu.VMEM((NZ, GROUP, B), f32),
+            pltpu.VMEM((2, SUBS + 1, SUBS, GROUP, B), f32),
             pltpu.VMEM((GROUP, 2 * NZ, B), f32),
             pltpu.VMEM((GROUP, 2 * NZ, B), f32),
             pltpu.VMEM((GROUP, SUBS, 1, WIDE), f32),
@@ -475,22 +495,21 @@
             pltpu.VMEM((NX, NB, E, B), f32),
             pltpu.VMEM((SUBS, 2, E, B), f32),
             pltpu.VMEM((2, NB, E, B), f32),
-            pltpu.VMEM((NB, CELLS + B, B), bf16),
-            pltpu.VMEM((NB, CELLS + B, B), bf16),
+            pltpu.VMEM((NB, CELLS + B, 2 * B), bf16),
             pltpu.VMEM((2 * E, CELLS), bf16),
             pltpu.VMEM((E, B), f32),
             pltpu.VMEM((B, B), f32),
             pltpu.VMEM((N_FLOW - 1, E, B), f32),
             pltpu.VMEM((N_FLOW - 2, B, B), f32),
-            pltpu.VMEM(((N_FLOW - 2) * B, B), bf16),
-            pltpu.VMEM(((N_FLOW - 2) * B, B), bf16),
+            pltpu.VMEM(((N_FLOW - 2) * B, 2 * B), bf16),
             pltpu.VMEM((N_FLOW - 2, 8, B), f32),
             pltpu.VMEM((2 * E, (N_FLOW - 2) * B), bf16),
             dma((8,)),
             dma((4, SUBS)), dma((4, SUBS)), dma((4, SUBS)), dma((4, SUBS)),
-            dma((NZ,)), dma((NZ,)), dma((GROUP,)), dma((GROUP,)),
+            dma((2, SUBS)), dma((2, SUBS)), dma((GROUP,)), dma((GROUP,)),
             dma((NX, SUBS)), dma((NX, SUBS)), dma((SUBS,)), dma((SUBS,)), dma((2, SUBS)), dma((2, SUBS)),
             dma((N_FLOW - 1,)), dma((N_FLOW - 1,)), dma((N_FLOW - 2,)), dma((N_FLOW - 2,)),
+            pltpu.SemaphoreType.REGULAR((3,)),
         ],
         compiler_params=pltpu.CompilerParams(collective_id=0, has_side_effects=True),
         name="transport_step",

time: 64 us -> 61.3 us (0.958)
  Pallas kernels: 62 us -> 59 us
    pallas_call x1, Pallas kernels: 62 us -> 59 us  [step(): pl.pallas_call(step_kernel, out_shape=[jax.ShapeDtypeStruct((E, NB, B), f...]
where the time goes in v4:
time: 61.3 us; the launch traced here: 60.8 us
  Pallas kernels  59 us (96%)
  other arithmetic  1.76 us (3%)
    pallas_call x1, Pallas kernels, step(): pl.pallas_call(step_kernel, out_shape=[jax.ShapeDtypeStruct((E, NB, B), f...  59 us
    broadcast_in_dim x1, other arithmetic, on_device(): step(upstream_block[0, 0], send_count[0, 0], conc_old[0, 0], face_flux[0,...  1.76 us

profile of v4, /device:TPU:56, one launch (start us, length us, event | category | flops | bytes accessed | tf_op | source)
XLA Modules:
  0.0 60.8 jit_solution(9065262043673505951)
XLA Ops:
  0.0 59.0 %transport_step.1 = (f32[64,8,128]{2,1,0:T(8,128)}, f32[64,8,128]{2,1,0:T(8,128)}) custom-call(s32[8]{0:T(128)} %bitcast.16, s32[64]{0:T(128)} %bitcast.17, f32[64,8,128]{2,1,0:T(8,128)} %bitcast.12, f32[8,128,128]{2,1,0:T(8,128)} %bitcast.10, f32[8,128,128]{2,1,0:T(8,128)} %bitcast.11, s32[64,128]{1,0:T(8,128)} %bitcast.13, s32[64,128]{1,0:T(8,128)} %bitcast.14, ...), custom_call_target="tpu_custom_call" | custom-call | tf_op jit(solution)/shard_map/transport_step/pallas_call | solution.py:470
  59.0 1.8 %add_bitcast_fusion = f32[1,1,64,8,128]{4,3,2,1,0:T(8,128)} fusion(f32[64,8,128]{2,1,0:T(8,128)} %get-tuple-element.7, f32[64,8,128]{2,1,0:T(8,128)} %get-tuple-element.8), kind=kLoop, calls=%fused_computation | loop fusion | flops 65536 | bytes 786432 | tf_op jit(solution)/shard_map/broadcast_in_dim | solution.py:521

commit v5 on v4

--- a/solution.py
+++ b/solution.py
@@ -106,23 +106,6 @@
     loads[0].wait()
     for b in range(NB):
         held[0, b] = conc_ref[:, b, :]
-    for load in loads[1:5]:
-        load.wait()
-    lane = lax.broadcasted_iota(jnp.int32, (1, B), 1)
-    for pz in range(NZ):
-        for g in range(GROUP):
-            peer_id = (g // NC) * NZ * NC + pz * NC + g % NC
-            row = send_ref[pl.ds(peer_id, 1), :]
-            live = jnp.where(lane < counts[peer_id], row, -1)
-            send_rows[pz, pl.ds(g, 1), :] = live.astype(jnp.float32)
-    for k in range(SUBS):
-        lists[0, 0, k] = send_rows[lax.rem(z + k + 1, NZ)]
-    for k in range(SUBS - 1):
-        lists[1, 0, k] = send_rows[lax.rem(z + NZ - k - 1, NZ)]
-    for g in range(GROUP):
-        rows = pl.ds((g // NC) * NZ * NC + g % NC, NZ, stride=NC)
-        recv_rows[g, pl.ds(0, NZ), :] = cells_ref[rows, :].astype(jnp.float32)
-        recv_rows[g, pl.ds(NZ, NZ), :] = coef_ref[rows, :]
 
     def right_copy(r, i):
         part = pl.ds(2 * i, 2)
@@ -248,12 +231,28 @@
     for i in range(SUBS):
         right_copy(0, i).start()
         left_copy(0, i).start()
-        if i == 0:
-            list_copy(0, 0).start()
-            list_copy(1, 0).start()
-            for dx, dc in group[1:]:
-                xmeta_copy(dx, dc).start()
     tell(0)
+    for load in loads[1:5]:
+        load.wait()
+    lane = lax.broadcasted_iota(jnp.int32, (1, B), 1)
+    for pz in range(NZ):
+        for g in range(GROUP):
+            peer_id = (g // NC) * NZ * NC + pz * NC + g % NC
+            row = send_ref[pl.ds(peer_id, 1), :]
+            live = jnp.where(lane < counts[peer_id], row, -1)
+            send_rows[pz, pl.ds(g, 1), :] = live.astype(jnp.float32)
+    for k in range(SUBS):
+        lists[0, 0, k] = send_rows[lax.rem(z + k + 1, NZ)]
+    for k in range(SUBS - 1):
+        lists[1, 0, k] = send_rows[lax.rem(z + NZ - k - 1, NZ)]
+    for g in range(GROUP):
+        rows = pl.ds((g // NC) * NZ * NC + g % NC, NZ, stride=NC)
+        recv_rows[g, pl.ds(0, NZ), :] = cells_ref[rows, :].astype(jnp.float32)
+        recv_rows[g, pl.ds(NZ, NZ), :] = coef_ref[rows, :]
+    list_copy(0, 0).start()
+    list_copy(1, 0).start()
+    for dx, dc in group[1:]:
+        xmeta_copy(dx, dc).start()
     for load in loads[5:]:
         load.wait()
     xmeta[0] = recv_rows[x * NC + c]
@@ -301,6 +300,14 @@
                     response_step(2 * i + 2)
                 pick(0, 0, i)
             else:
+                if r == 2:
+                    @pl.when(i == 1)
+                    def _():
+                        pl.semaphore_wait(rounds.at[2], 2)
+                    for k in range(1, N_FLOW - 1):
+                        @pl.when((i == 1) & (flow >= 1) & (flow + k < N_FLOW))
+                        def _(k=k):
+                            pass_copy(k).start()
                 pick(r - 1, 0, i)
                 pick(NZ - r + 1, 1, i)
                 deposit_all(i, r - 2)
@@ -312,12 +319,6 @@
                             + resp[NB - 1, pl.ds(CELLS, B), pl.ds(B, B)].astype(jnp.float32))
             pl.semaphore_wait(rounds.at[1], 2)
             tell(2)
-        if r == 2:
-            pl.semaphore_wait(rounds.at[2], 2)
-            for k in range(1, N_FLOW - 1):
-                @pl.when((flow >= 1) & (flow + k < N_FLOW))
-                def _(k=k):
-                    pass_copy(k).start()
 
     list_copy(0, 3).wait_recv()
     load_lhs(3, 0)
@@ -326,19 +327,22 @@
     def late(p, carry):
         pick(3, 0, p)
         pick(5, 1, p)
-        deposit_all(p, 2)
         return carry
 
     lax.fori_loop(0, SUBS, late, 0)
+    deposit_all(2, 2)
     for i in range(2):
         right_copy(3, i).wait_recv()
         left_copy(3, i + 2).wait_recv()
     load_lhs(4, 0)
 
     def finish(p, q):
-        deposit(p, 1, 3, q)
+        left_over = (3,) if p == 2 else (2, 3)
+        for t in left_over:
+            deposit(p, 1, t, q)
         pair_copy(p, q).start()
-        deposit(p, 0, 3, q)
+        for t in left_over:
+            deposit(p, 0, t, q)
 
     def combine(p, q):
         pair_copy(p, q).wait_recv()

time: 61.3 us -> 63.3 us (1.033)
  Pallas kernels: 59 us -> 61.2 us
    pallas_call x1, Pallas kernels: 59 us -> 61.2 us  [step(): pl.pallas_call(step_kernel, out_shape=[jax.ShapeDtypeStruct((E, NB, B), f...]
where the time goes in v5:
time: 63.3 us; the launch traced here: 63 us
  Pallas kernels  61.2 us (97%)
  other arithmetic  1.76 us (3%)
    pallas_call x1, Pallas kernels, step(): pl.pallas_call(step_kernel, out_shape=[jax.ShapeDtypeStruct((E, NB, B), f...  61.2 us
    broadcast_in_dim x1, other arithmetic, on_device(): step(upstream_block[0, 0], send_count[0, 0], conc_old[0, 0], face_flux[0,...  1.76 us

profile of v5, /device:TPU:56, one launch (start us, length us, event | category | flops | bytes accessed | tf_op | source)
XLA Modules:
  0.0 63.0 jit_solution(2468546275024924687)
XLA Ops:
  0.0 61.2 %transport_step.1 = (f32[64,8,128]{2,1,0:T(8,128)}, f32[64,8,128]{2,1,0:T(8,128)}) custom-call(s32[8]{0:T(128)} %bitcast.16, s32[64]{0:T(128)} %bitcast.17, f32[64,8,128]{2,1,0:T(8,128)} %bitcast.12, f32[8,128,128]{2,1,0:T(8,128)} %bitcast.10, f32[8,128,128]{2,1,0:T(8,128)} %bitcast.11, s32[64,128]{1,0:T(8,128)} %bitcast.13, s32[64,128]{1,0:T(8,128)} %bitcast.14, ...), custom_call_target="tpu_custom_call" | custom-call | tf_op jit(solution)/shard_map/transport_step/pallas_call | solution.py:474
  61.2 1.8 %add_bitcast_fusion = f32[1,1,64,8,128]{4,3,2,1,0:T(8,128)} fusion(f32[64,8,128]{2,1,0:T(8,128)} %get-tuple-element.7, f32[64,8,128]{2,1,0:T(8,128)} %get-tuple-element.8), kind=kLoop, calls=%fused_computation | loop fusion | flops 65536 | bytes 786432 | tf_op jit(solution)/shard_map/broadcast_in_dim | solution.py:525
